TPU v7x, 32 devices: a whole 2x2x4 slice. The times are simulated.
32 devices in a mesh: pen: 16 (over z, x, core), coil: 2 (over y).
Axes of the slice: x: 2, y: 2, z: 4, core: 2. Of those that a mesh axis runs over, the one named last changes fastest.
Arguments:
- image_field: float32 [512, 512, 2, 128], P('pen'), may hold values from -6 to 6
- coil_maps: bfloat16 [2, 512, 512, 2, 128], P('coil', 'pen'), may hold values from -5 to 5
- samples: bfloat16 [2, 4096, 128, 2, 128], P('coil', 'pen'), may hold values from -6 to 6
- kernels: bfloat16 [4096, 128, 128], P('pen'), may hold values from -0.5 to 0.5
- tile_of_block: int32 [4096], P('pen'), may hold values from 0 to 2047, as said below
Outputs:
- gradient: float32 [512, 512, 2, 128], P('pen', 'coil')
Inputs may be any that keep to these rules, and one draw needn't show every extreme that they name: The tile of every block lies with the block: tile_of_block[b] // 128 == b // 256; every tile is named by at least one block.
All inputs are finite; a program needn't handle non-finite values.
Results may differ from a plain program's by a relative error of at most 0.012.
Values may be sent and summed in bfloat16 or wider, within the bound.
No kernel may reach another device: no remote copies, remote signals or barrier semaphores. Data moves between devices by JAX's collectives and lax.ppermute only.
A program may use at most 256 MiB of HBM per device.

v0:
```python
import math

import jax
import jax.numpy as jnp
from jax import lax
from jax.sharding import PartitionSpec as P

NL = 512
NZ = 128
TILE = 128


tv_weight = 2.0


def shifted(shard, axis, by):
    length = lax.axis_size(axis)
    pairs = [(i, i + by) for i in range(length) if 0 <= i + by < length]
    return lax.ppermute(shard, axis, pairs)


def dft_tables(length, direction):
    index = lax.iota(jnp.int32, length)
    phase = index[:, None] * index[None, :] % length
    angle = 2.0 * math.pi / length * phase.astype(jnp.float32)
    cosine = jnp.cos(angle) / math.sqrt(length)
    sine = direction * jnp.sin(angle) / math.sqrt(length)
    table = jnp.stack([jnp.stack([cosine, sine], -1), jnp.stack([-sine, cosine], -1)], 1)
    high_part = table.astype(jnp.bfloat16)
    low_part = (table - high_part.astype(jnp.float32)).astype(jnp.bfloat16)
    return (high_part, low_part)


def along_second(tables, values):
    first = jnp.einsum("kpxr,yxrz->ykpz", tables[0], values, preferred_element_type=jnp.float32)
    return first + jnp.einsum(
        "kpxr,yxrz->ykpz", tables[1], values, preferred_element_type=jnp.float32
    )


def along_first(tables, values):
    first = jnp.einsum("kpyr,yxrz->kxpz", tables[0], values, preferred_element_type=jnp.float32)
    return first + jnp.einsum(
        "kpyr,yxrz->kxpz", tables[1], values, preferred_element_type=jnp.float32
    )


def flux_fields(extended, first_row, first_col):
    center = extended[:-1, :-1]
    row_ids = first_row + jnp.arange(center.shape[0])
    col_ids = first_col + jnp.arange(center.shape[1])
    diff_y = (extended[1:, :-1] - center) * (row_ids != NL - 1)[:, None, None, None]
    diff_x = (extended[:-1, 1:] - center) * (col_ids != NL - 1)[None, :, None, None]
    diff_z = jnp.concatenate(
        [center[..., 1:] - center[..., :-1], jnp.zeros_like(center[..., :1])], 3
    )
    norm_den = jnp.sqrt(
        1.0 + jnp.sum(diff_y * diff_y + diff_x * diff_x + diff_z * diff_z, axis=2, keepdims=True)
    )
    inside = ((row_ids >= 0)[:, None] & (col_ids >= 0)[None, :]).astype(jnp.float32)[
        :, :, None, None
    ]
    return (diff_y / norm_den * inside, diff_x / norm_den * inside, diff_z / norm_den * inside)


def plane_divergence(flux_z):
    return jnp.concatenate([jnp.zeros_like(flux_z[..., :1]), flux_z[..., :-1]], 3) - flux_z


def on_device(image_field, coil_maps, samples, kernels, tile_of_block):
    own_rows = image_field.shape[0]
    pen_count = lax.axis_size("pen")
    half_cols = NL // lax.axis_size("coil")
    local_cols = NL // pen_count
    pen_id = lax.axis_index("pen")
    coil_id = lax.axis_index("coil")
    row_start = pen_id * own_rows
    col_start = coil_id * half_cols
    map_real = coil_maps[0, :, :, 0].astype(jnp.float32)
    map_imag = coil_maps[0, :, :, 1].astype(jnp.float32)
    field_real = image_field[:, :, 0]
    field_imag = image_field[:, :, 1]
    coil_image = jnp.stack(
        [
            map_real * field_real - map_imag * field_imag,
            map_real * field_imag + map_imag * field_real,
        ],
        2,
    ).astype(jnp.bfloat16)
    forward_tab = dft_tables(NL, 1.0)
    adjoint_tab = dft_tables(NL, -1.0)
    rows_spectrum = along_second(forward_tab, coil_image).astype(jnp.bfloat16)
    kspace_grid = along_first(
        forward_tab, lax.all_to_all(rows_spectrum, "pen", split_axis=1, concat_axis=0, tiled=True)
    ).astype(jnp.bfloat16)
    grid_tiles = (
        kspace_grid.reshape(NL // TILE, TILE, local_cols, 2 * NZ)
        .transpose(2, 0, 1, 3)
        .reshape(-1, TILE, 2 * NZ)
    )
    tile_count = grid_tiles.shape[0]
    local_ids = tile_of_block - pen_id * tile_count
    picked = jnp.take(grid_tiles, local_ids, axis=0)
    predicted = jnp.einsum("bst,btc->bsc", kernels, picked, preferred_element_type=jnp.float32)
    measured = samples[0].reshape(predicted.shape).astype(jnp.float32)
    misfit = (predicted - measured).astype(jnp.bfloat16)
    back_terms = jnp.einsum("bst,bsc->btc", kernels, misfit, preferred_element_type=jnp.float32)
    onehot = (local_ids[:, None] == jnp.arange(tile_count, dtype=jnp.int32)[None, :]).astype(
        jnp.float32
    )
    back_tiles = jnp.einsum(
        "bl,btc->ltc", onehot, back_terms, precision=lax.Precision.HIGHEST
    ).astype(jnp.bfloat16)
    back_grid = (
        back_tiles.reshape(local_cols, NL // TILE, TILE, 2 * NZ)
        .transpose(1, 2, 0, 3)
        .reshape(NL, local_cols, 2, NZ)
    )
    back_rows = along_first(adjoint_tab, back_grid).astype(jnp.bfloat16)
    back_image = along_second(
        adjoint_tab, lax.all_to_all(back_rows, "pen", split_axis=0, concat_axis=1, tiled=True)
    )
    back_real = back_image[:, :, 0]
    back_imag = back_image[:, :, 1]
    coil_term = jnp.stack(
        [map_real * back_real + map_imag * back_imag, map_real * back_imag - map_imag * back_real],
        2,
    )
    summed = lax.psum(coil_term, "coil")
    data_gradient = lax.dynamic_slice_in_dim(summed, col_start, half_cols, 1)
    padded = jnp.pad(image_field, ((0, 0), (1, 1), (0, 0), (0, 0)))
    window = lax.dynamic_slice_in_dim(padded, col_start, half_cols + 2, 1)
    upper_row = shifted(window[:1], "pen", -1)
    extended = jnp.concatenate([window, upper_row], 0)
    flux_y, flux_x, flux_z = flux_fields(extended, row_start, col_start - 1)
    lower_row = shifted(flux_y[-1:], "pen", 1)
    flux_before = jnp.concatenate([lower_row, flux_y[:-1]], 0)
    tv_part = (
        flux_before[:, 1:]
        - flux_y[:, 1:]
        + flux_x[:, :-1]
        - flux_x[:, 1:]
        + plane_divergence(flux_z[:, 1:])
    )
    return data_gradient + tv_weight * tv_part


def solution(mesh):
    in_specs = (
        P("pen", None, None, None),
        P("coil", "pen", None, None, None),
        P("coil", "pen", None, None, None),
        P("pen", None, None),
        P("pen"),
    )
    out_specs = P("pen", "coil", None, None)
    return jax.shard_map(
        on_device, mesh=mesh, in_specs=in_specs, out_specs=out_specs, check_vma=False
    )
```

profile of v0, /device:TPU:0, one launch (start us, length us, event | category | flops | bytes accessed | tf_op | source)
XLA Modules:
  0.0 1350.3 jit_solution(1019381093489078857)
XLA Ops:
  20.2 25.0 %copy.32 = f32[32,512,2,128]{1,3,2,0:T(8,128)} copy(f32[32,512,2,128]{3,2,1,0:T(2,128)} %param.5) | data formatting | bytes 33554432 | tf_op args[0]
  45.2 17.5 %fusion.90 = (bf16[1,32,512,1,128]{4,3,2,1,0:T(2,128)(2,1)}, bf16[1,32,512,1,128]{4,3,2,1,0:T(2,128)(2,1)}) fusion(bf16[1,32,512,2,128]{4,3,2,1,0:T(2,128)(2,1)} %param.6), kind=kLoop, calls=%fused_computation.127 | loop fusion | bytes 16777216 | tf_op jit(solution)/shard_map/slice | solution.py:79
  62.7 18.3 %copy.75 = bf16[1,32,512,1,128]{2,4,1,3,0:T(8,128)(2,1)} copy(bf16[1,32,512,1,128]{4,3,2,1,0:T(2,128)(2,1)} %get-tuple-element.13) | data formatting | bytes 8388608
  81.0 18.3 %copy.76 = bf16[1,32,512,1,128]{2,4,1,3,0:T(8,128)(2,1)} copy(bf16[1,32,512,1,128]{4,3,2,1,0:T(2,128)(2,1)} %get-tuple-element.14) | data formatting | bytes 8388608
  126.7 17.4 %fusion.37 = bf16[32,512,2,128]{1,3,2,0:T(8,128)(2,1)} fusion(bf16[32,512,1,128]{1,3,2,0:T(8,128)(2,1)} %copy-done.4, bf16[32,512,1,128]{1,3,2,0:T(8,128)(2,1)} %copy-done.3, f32[32,128,512,2,1]{2,1,4,3,0:T(8,128)} %fusion.36, f32[512,1,512,2]{2,0,3,1:T(8,128)} %copy-done.8, f32[512,1,512,2]{2,0,3,1:T(8,128)} %copy-done.10), kind=kOutput, calls=%fused_computation.63 | convolution fusion | flops 8620343296 | bytes 37748736 | tf_op jit(solution)/shard_map/kpxr,yxrz->ykpz/dot_general | solution.py:36
  144.1 21.3 %copy.35 = bf16[32,512,2,128]{3,2,0,1:T(2,128)(2,1)} copy(bf16[32,512,2,128]{1,3,2,0:T(8,128)(2,1)} %fusion.37) | data formatting | bytes 16777216 | tf_op jit(solution)/shard_map/convert_element_type | solution.py:92
  172.9 45.1 %copy.42 = f32[1,256,128,2,128]{2,4,3,1,0:T(8,128)} copy(bf16[1,256,128,2,128]{4,3,2,1,0:T(2,128)(2,1)} %param.7) | data formatting | bytes 50331648 | tf_op jit(solution)/shard_map/convert_element_type | solution.py:105
  218.0 105.4 %all-to-all-done = bf16[32,512,2,128]{3,2,0,1:T(2,128)(2,1)} async-done(((bf16[32,512,2,128]{3,2,0,1:T(2,128)(2,1)}), bf16[32,512,2,128]{3,2,0,1:T(2,128)(2,1)}, u32[]{:S(2)}, u32[]{:S(2)}) %all-to-all-start) | async-done | bytes 8388640 | tf_op jit(solution)/shard_map/all_to_all | solution.py:94
  323.4 16.5 %copy.36 = bf16[32,512,2,128]{3,1,2,0:T(8,128)(2,1)} copy(bf16[32,512,2,128]{3,2,0,1:T(2,128)(2,1)} %all-to-all-done) | data formatting | bytes 16777216 | tf_op jit(solution)/shard_map/all_to_all | solution.py:94
  349.2 14.0 %copy.55 = bf16[512,32,2,128,1]{0,3,2,4,1:T(8,128)(2,1)} copy(bf16[512,32,2,128,1]{3,1,2,0,4:T(8,128)(2,1)} %bitcast.154) | data formatting | bytes 16777216 | tf_op jit(solution)/shard_map/all_to_all | solution.py:94
  363.2 16.4 %fusion.68 = f32[32,128,512,2,1]{2,1,4,3,0:T(8,128)} fusion(bf16[512,32,2,128,1]{0,3,2,4,1:T(8,128)(2,1)} %copy.55, f32[512,1,512,2]{2,0,3,1:T(8,128)S(1)} %copy-done.9, f32[512,1,512,2]{2,0,3,1:T(8,128)} %copy-done.10), kind=kOutput, calls=%fused_computation.100 | convolution fusion | flops 8594128896 | bytes 29360128 | tf_op jit(solution)/shard_map/kpyr,yxrz->kxpz/dot_general | solution.py:42
  379.7 17.1 %fusion.38 = bf16[512,32,2,128]{0,3,2,1:T(8,128)(2,1)} fusion(bf16[512,32,2,128,1]{0,3,2,4,1:T(8,128)(2,1)} %copy.55, f32[32,128,512,2,1]{2,1,4,3,0:T(8,128)} %fusion.68, f32[512,1,512,2]{2,0,3,1:T(8,128)S(1)} %copy-done.9, f32[512,1,512,2]{2,0,3,1:T(8,128)S(1)} %copy-done.11), kind=kOutput, calls=%fused_computation.64 | convolution fusion | flops 8603566080 | bytes 37748736 | tf_op jit(solution)/shard_map/kpyr,yxrz->kxpz/dot_general | solution.py:43
  409.2 13.3 copy.40
  422.5 13.2 gather_fusion
  435.7 38.4 %fusion.10 = f32[256,128,256]{1,2,0:T(8,128)} fusion(bf16[256,128,128]{2,1,0:T(8,128)(2,1)} %param.8, f32[256,128,256]{1,2,0:T(8,128)} %bitcast.151, bf16[256,128,256]{2,1,0:T(8,128)(2,1)} %gather_fusion, pred[256]{0:T(512)(128)(4,1)S(1)} %get-tuple-element.5), kind=kOutput, calls=%fused_computation.30 | convolution fusion | flops 4320133120 | bytes 92274944 | tf_op jit(solution)/shard_map/bst,bsc->btc/dot_general | solution.py:107
  474.1 33.4 %copy.43 = f32[256,128,256]{2,0,1:T(8,128)} copy(f32[256,128,256]{1,2,0:T(8,128)} %fusion.10) | data formatting | bytes 67108864 | tf_op jit(solution)/shard_map/bst,bsc->btc/dot_general | solution.py:107
  507.5 20.8 %convolution_convert_fusion = bf16[128,128,256]{2,0,1:T(8,128)(2,1)} fusion(f32[256,128,256]{2,0,1:T(8,128)} %copy.43, s32[256]{0:T(256)S(1)} %get-tuple-element.6), kind=kOutput, calls=%fused_computation.60 | convolution fusion | flops 12889128960 | bytes 41944064 | tf_op jit(solution)/shard_map/bl,btc->ltc/dot_general | solution.py:111
  540.8 18.0 %copy.44 = bf16[4,128,32,256]{1,0,3,2:T(4,128)(2,1)} copy(bf16[4,128,32,256]{3,0,2,1:T(4,128)(2,1)} %bitcast.155) | data formatting | bytes 16777216 | tf_op jit(solution)/shard_map/transpose | solution.py:116
  558.9 13.2 reshape.238
  572.1 16.8 %fusion.32 = f32[32,128,512,2,1]{2,1,4,3,0:T(8,128)} fusion(bf16[512,32,2,128,1]{0,3,2,1,4:T(8,128)(2,1)} %reshape.238, f32[512,1,512,2]{2,0,3,1:T(8,128)} %get-tuple-element.17, f32[512,1,512,2]{2,0,3,1:T(8,128)S(1)} %copy-done.5), kind=kOutput, calls=%fused_computation.57 | convolution fusion | flops 8594128896 | bytes 29360128 | tf_op jit(solution)/shard_map/kpyr,yxrz->kxpz/dot_general | solution.py:42
  588.9 16.9 %fusion.39 = bf16[512,32,2,128]{0,3,2,1:T(8,128)(2,1)} fusion(bf16[512,32,2,128,1]{0,3,2,1,4:T(8,128)(2,1)} %reshape.238, f32[32,128,512,2,1]{2,1,4,3,0:T(8,128)} %fusion.32, f32[512,1,512,2]{2,0,3,1:T(8,128)S(1)} %copy-done.6, f32[512,1,512,2]{2,0,3,1:T(8,128)S(1)} %copy-done.5), kind=kOutput, calls=%fused_computation.65 | convolution fusion | flops 8603566080 | bytes 37748736 | tf_op jit(solution)/shard_map/kpyr,yxrz->kxpz/dot_general | solution.py:43
  605.8 21.2 %copy.45 = bf16[512,32,2,128]{3,2,1,0:T(2,128)(2,1)} copy(bf16[512,32,2,128]{0,3,2,1:T(8,128)(2,1)} %fusion.39) | data formatting | bytes 16777216 | tf_op jit(solution)/shard_map/convert_element_type | solution.py:119
  627.1 218.8 %all_to_all.36 = bf16[512,32,2,128]{3,2,1,0:T(2,128)(2,1)} all-to-all(bf16[512,32,2,128]{3,2,1,0:T(2,128)(2,1)} %copy.45), channel_id=1, replica_groups=mesh['pen'=16,'coil'=2] {'pen'}, dimensions={0} | all-to-all | bytes 16777216 | tf_op jit(solution)/shard_map/all_to_all | solution.py:121
  863.8 14.8 %fusion.65 = f32[32,128,512,2,1]{2,1,4,3,0:T(8,128)} fusion(bf16[32,512,2,128,1]{3,1,2,4,0:T(8,128)(2,1)} %bitcast.157, f32[512,1,512,2]{2,0,3,1:T(8,128)S(1)} %copy-done.7, f32[512,1,512,2]{2,0,3,1:T(8,128)S(1)} %copy-done.5), kind=kOutput, calls=%fused_computation.99 | convolution fusion | flops 8594128896 | bytes 29360128 | tf_op jit(solution)/shard_map/kpxr,yxrz->ykpz/dot_general | solution.py:35
  878.6 19.0 %fusion.3 = f32[32,512,2,128]{1,3,2,0:T(8,128)} fusion(f32[32,128,512,2,1]{2,1,4,3,0:T(8,128)} %fusion.65, bf16[32,512,2,128,1]{3,1,2,4,0:T(8,128)(2,1)} %bitcast.158, f32[512,1,512,2]{2,0,3,1:T(8,128)} %get-tuple-element.17, f32[512,1,512,2]{2,0,3,1:T(8,128)S(1)} %copy-done.5), kind=kOutput, calls=%fused_computation.12 | convolution fusion | flops 8599371776 | bytes 46137344 | tf_op jit(solution)/shard_map/kpxr,yxrz->ykpz/dot_general | solution.py:36
  924.4 13.1 pad_dynamic-slice_fusion.5
  937.5 21.1 %fusion.15 = f32[32,257,2,127]{1,3,2,0:T(8,128)} fusion(s32[]{:T(128)S(6)} %select_n.65, s32[]{:T(128)S(6)} %add.172, f32[32,512,2,128]{1,3,2,0:T(8,128)} %copy.32), kind=kLoop, calls=%fused_computation.33 | loop fusion | flops 2088896 | bytes 25132808 | tf_op jit(solution)/shard_map/sub | solution.py:55
  958.7 23.7 %add_reduce_fusion = f32[32,257,128]{1,2,0:T(8,128)} fusion(f32[32,257,2,127]{1,3,2,0:T(8,128)} %fusion.15, f32[257]{0:T(512)S(1)} %get-tuple-element.21, s32[]{:T(128)S(6)} %select_n.65, f32[32,512,2,128]{1,3,2,0:T(8,128)} %copy.32, s32[]{:T(128)S(6)} %add.171, f32[32]{0:T(128)S(1)} %get-tuple-element.22, f32[1,258,2,128]{1,3,2,0:T(8,128)S(1)} %collective-permute-done, ...), kind=kLoop, calls=%fused_computation.40 | loop fusion | flops 22106112 | bytes 38062988 | tf_op jit(solution)/shard_map/reduce_sum | solution.py:58
  986.8 39.5 %divide_multiply_fusion.2 = (f32[32,257,2,128]{1,3,2,0:T(8,128)}, f32[32,257,2,128]{1,3,2,0:T(8,128)}, f32[32,257,2,128]{1,3,2,0:T(8,128)}) fusion(f32[32,257]{1,0:T(8,128)S(1)} %and_convert_fusion, f32[32,257,128]{1,2,0:T(8,128)S(1)} %add_sqrt_fusion, f32[32]{0:T(128)S(1)} %get-tuple-element.22, s32[]{:T(128)S(6)} %select_n.65, ...), kind=kLoop, calls=%fused_computation.39 | loop fusion | flops 23158784 | bytes 63360012 | tf_op jit(solution)/shard_map/mul | solution.py:63
  1050.2 250.9 %all-reduce.5.cloned.1.call-done = f32[32,512,2,128]{1,3,2,0:T(8,128)} async-done(((f32[32,512,2,128]{1,3,2,0:T(8,128)}), f32[32,512,2,128]{1,3,2,0:T(8,128)}) %all-reduce.5.cloned.1.call-update) | async-done | bytes 16777232 | tf_op jit(solution)/shard_map/psum | solution.py:129
  1301.1 28.7 %fusion.30 = f32[32,256,2,128]{1,3,2,0:T(8,128)} fusion(f32[32,257,2,128]{1,3,2,0:T(8,128)} %get-tuple-element.15, f32[32,257,2,128]{1,3,2,0:T(8,128)} %get-tuple-element.12, f32[32,257,2,128]{1,3,2,0:T(8,128)} %get-tuple-element.11, f32[31,257,2,128]{1,3,2,0:T(8,128)} %slice.90, f32[1,257,2,128]{1,3,2,0:T(8,128)S(1)} %collective-permute-done.1, ...), kind=kLoop, calls=%fused_computation.50 | loop fusion | flops 16777216 | bytes 67076100 | tf_op jit(solution)/shard_map/add | solution.py:145
  1329.8 13.1 copy.51
  (57 shorter events, 156.1 us)
Async XLA Ops:
  99.3 10.2 copy-start.1
  99.3 10.2 copy-start.2
  109.4 3.3 copy-start.3
  109.4 4.4 copy-start.4
  112.6 1.9 copy-start.8
  112.6 2.6 copy-start.10
  165.4 158.0 %all-to-all-start = ((bf16[32,512,2,128]{3,2,0,1:T(2,128)(2,1)}), bf16[32,512,2,128]{3,2,0,1:T(2,128)(2,1)}, u32[]{:S(2)}, u32[]{:S(2)}) async-start(bf16[32,512,2,128]{3,2,0,1:T(2,128)(2,1)} %copy.35), calls=%async_computation | async-start | bytes 16777216 | tf_op jit(solution)/shard_map/all_to_all | solution.py:94
  172.9 1128.3 %all-reduce.5.cloned.1.call-start = ((), (), s32[]{:S(2)}) async-start(), calls=%async_computation.2 | async-start | bytes 33554432 | tf_op jit(solution)/shard_map/psum | solution.py:129
  172.9 45.1 %copy-start.12 = (s32[256]{0:T(256)S(1)}, s32[256]{0:T(256)}, u32[]{:S(2)}) copy-start(s32[256]{0:T(256)} %param.9) | copy-start | bytes 3076
  349.2 14.0 %copy-start.9 = (f32[512,1,512,2]{2,0,3,1:T(8,128)S(1)}, f32[512,1,512,2]{2,0,3,1:T(8,128)}, u32[]{:S(2)}) copy-start(f32[512,1,512,2]{2,0,3,1:T(8,128)} %copy-done.8) | copy-start | bytes 6291460
  363.2 16.4 %copy-start.11 = (f32[512,1,512,2]{2,0,3,1:T(8,128)S(1)}, f32[512,1,512,2]{2,0,3,1:T(8,128)}, u32[]{:S(2)}) copy-start(f32[512,1,512,2]{2,0,3,1:T(8,128)} %copy-done.10) | copy-start | bytes 6291460
  558.9 13.2 copy-start.5
  572.1 16.8 %copy-start.6 = (f32[512,1,512,2]{2,0,3,1:T(8,128)S(1)}, f32[512,1,512,2]{2,0,3,1:T(8,128)}, u32[]{:S(2)}) copy-start(f32[512,1,512,2]{2,0,3,1:T(8,128)} %get-tuple-element.17) | copy-start | bytes 6291460
  854.7 9.1 copy-start.7
  878.6 19.0 %copy-start = (bf16[1,32,512,1,128]{2,4,1,3,0:T(8,128)(2,1)S(1)}, bf16[1,32,512,1,128]{2,4,1,3,0:T(8,128)(2,1)}, u32[]{:S(2)}) copy-start(bf16[1,32,512,1,128]{2,4,1,3,0:T(8,128)(2,1)} %copy.75) | copy-start | bytes 12582916
  923.1 35.6 %collective-permute-start = (f32[1,258,2,128]{1,3,2,0:T(8,128)S(1)}, f32[1,258,2,128]{1,3,2,0:T(8,128)S(1)}, u32[]{:S(2)}, u32[]{:S(2)}) collective-permute-start(f32[1,258,2,128]{1,3,2,0:T(8,128)S(1)} %pad_dynamic-slice_fusion.4), channel_id=1, source_target_pairs={{2,0},{4,2},{6,4},{8,6},{10,8},{12,10},{14,12},{16,14},{18,16},{20... | collective-permute-start | bytes 792584 | tf_op jit(solution)/shard_map/ppermute | solution.py:19
  1027.3 23.0 %collective-permute-start.1 = (f32[1,257,2,128]{1,3,2,0:T(8,128)S(1)}, f32[1,257,2,128]{1,3,2,0:T(8,128)S(1)}, u32[]{:S(2)}, u32[]{:S(2)}) collective-permute-start(f32[1,257,2,128]{1,3,2,0:T(8,128)S(1)} %slice.89), channel_id=1, source_target_pairs={{0,2},{2,4},{4,6},{6,8},{8,10},{10,12},{12,14},{14,16},{16,18},{18... | collective-permute-start | bytes 789512 | tf_op jit(solution)/shard_map/ppermute | solution.py:19
Sparse Core Ops, SparseCore 0:
  922.0 379.1 all-reduce.4
where the time goes:
time: 1360 us; the launch traced here: 1350 us
  local copies, waits for them, and re-layouts  393 us (29%)
  waiting for transfers between devices  356 us (26%)
  blocking collectives  219 us (16%)
  matrix products  189 us (14%)
  other arithmetic  169 us (12%)
  between operations  14.1 us (1%)
    psum x1, waiting for transfers between devices, on_device(): summed = lax.psum(coil_term, 'coil')  251 us
    all_to_all x1, blocking collectives, on_device(): lax.all_to_all(back_rows, 'pen', split_axis=0, concat_axis=1, tiled=True)  219 us
    all_to_all x1, waiting for transfers between devices, on_device(): lax.all_to_all(rows_spectrum, 'pen', split_axis=1, concat_axis=0, tiled=T...  105 us
    unnamed x29, local copies, waits for them, and re-layouts  64.2 us
    convert_element_type x1, local copies, waits for them, and re-layouts, on_device(): measured = samples[0].reshape(predicted.shape).astype(jnp.float32)  45.1 us
    all_to_all x3, local copies, waits for them, and re-layouts, on_device(): lax.all_to_all(rows_spectrum, 'pen', split_axis=1, concat_axis=0, tiled=T...  39.8 us
    mul x1, other arithmetic, flux_fields(): diff_y / norm_den * inside  39.5 us
    dot_general x1, matrix products, on_device(): jnp.einsum('bst,bsc->btc', kernels, misfit, preferred_element_type=jnp.fl...  38.4 us
  transfers between devices with their start and end apart: 4, of which 2 were waited for; matrix products, arithmetic and copies ran while one was open for 13% of the time, Pallas kernels for 0%

commit v1 on v0

--- a/solution.py
+++ b/solution.py
@@ -1,8 +1,14 @@
+import functools
 import math
+
+import numpy
 
 import jax
 import jax.numpy as jnp
 from jax import lax
+from jax.experimental import pallas as pl
+from jax.experimental.pallas import tpu as pltpu
+
 from jax.sharding import PartitionSpec as P
 
 NL = 512
@@ -145,6 +151,577 @@
     return data_gradient + tv_weight * tv_part
 
 
+def pair_tables(scale, row_order, col_order):
+    phase = numpy.outer(row_order, col_order) % NL
+    angle = 2.0 * math.pi / NL * phase
+    return (
+        jnp.asarray(numpy.cos(angle) * scale, jnp.bfloat16),
+        jnp.asarray(numpy.sin(angle) * scale, jnp.bfloat16),
+    )
+
+
+def mxu(left, right):
+    return jnp.dot(left, right, preferred_element_type=jnp.float32)
+
+
+def rows_kernel(image_ref, maps_ref, cos_ref, sin_ref, out_ref, map_scr, spec_scr):
+    half = pl.program_id(1)
+    out_rows = cos_ref.shape[0]
+    cosine = cos_ref[...]
+    sine = sin_ref[...]
+    for pair in range(4):
+        reals, imags = [], []
+        for row in (2 * pair, 2 * pair + 1):
+            map_scr[row] = maps_ref[row].astype(jnp.float32)
+            map_real = map_scr[row, pl.ds(0, NL, 2), :]
+            map_imag = map_scr[row, pl.ds(1, NL, 2), :]
+            field_real = image_ref[row, pl.ds(0, NL, 2), :]
+            field_imag = image_ref[row, pl.ds(1, NL, 2), :]
+            reals.append((map_real * field_real - map_imag * field_imag).astype(jnp.bfloat16))
+            imags.append((map_real * field_imag + map_imag * field_real).astype(jnp.bfloat16))
+        real = jnp.concatenate(reals, 1)
+        imag = jnp.concatenate(imags, 1)
+        spec_real = mxu(cosine, real) + mxu(sine, imag)
+        spec_imag = mxu(cosine, imag) - mxu(sine, real)
+        for sub in range(2):
+            base = pl.multiple_of((half * 8 + 2 * pair + sub) * 2 * out_rows, 2 * out_rows)
+            lanes = slice(sub * NZ, (sub + 1) * NZ)
+            spec_scr[pl.ds(base, out_rows), :] = spec_real[:, lanes]
+            spec_scr[pl.ds(base + out_rows, out_rows), :] = spec_imag[:, lanes]
+
+    @pl.when(half == 1)
+    def _():
+        def move(step, carry):
+            for sub in range(8):
+                col = step * 8 + sub
+                for part in range(2):
+                    start = part * out_rows + col
+                    low = spec_scr[pl.ds(start, 8, 2 * out_rows), :]
+                    high = spec_scr[pl.ds(start + 16 * out_rows, 8, 2 * out_rows), :]
+                    out_ref[2 * col + part] = jnp.concatenate([low, high], 0).astype(jnp.bfloat16)
+            return carry
+
+        lax.fori_loop(0, out_rows // 8, move, 0)
+
+
+def row_spectra(image, maps, tables, chunk, chunks):
+    rows = image.shape[0]
+    out_rows = NL // chunks
+    return pl.pallas_call(
+        rows_kernel,
+        grid=(rows // 16, 2),
+        in_specs=[
+            pl.BlockSpec((8, 2 * NL, NZ), lambda i, h: (2 * i + h, 0, 0)),
+            pl.BlockSpec((8, 2 * NL, NZ), lambda i, h: (2 * i + h, 0, 0)),
+            pl.BlockSpec((out_rows, NL), lambda i, h: (chunk, 0)),
+            pl.BlockSpec((out_rows, NL), lambda i, h: (chunk, 0)),
+        ],
+        out_specs=pl.BlockSpec((2 * out_rows, 16, NZ), lambda i, h: (0, i, 0)),
+        out_shape=jax.ShapeDtypeStruct((2 * out_rows, rows, NZ), jnp.bfloat16),
+        scratch_shapes=[
+            pltpu.VMEM((8, 2 * NL, NZ), jnp.float32),
+            pltpu.VMEM((16 * 2 * out_rows, NZ), jnp.float32),
+        ],
+        cost_estimate=pl.CostEstimate(
+            flops=8 * rows * out_rows * NL * NZ, bytes_accessed=30000000, transcendentals=0
+        ),
+    )(image, maps, *tables)
+
+
+DEPTH = 8
+
+
+def columns_kernel(
+    first_group,
+    order_ref,
+    local_ref,
+    bounds_ref,
+    spec_ref,
+    cos_ref,
+    sin_ref,
+    kernels_ref,
+    samples_ref,
+    *rest,
+):
+    row_chunks = len(rest) - 10
+    outs = rest[:row_chunks]
+    tiles, sums, backs, sample_scr, moved, kernel_buf, sample_buf, kernel_sem, sample_sem, _ = rest[
+        row_chunks:
+    ]
+    step = pl.program_id(0)
+    steps = pl.num_programs(0)
+    first = bounds_ref[first_group]
+    last = bounds_ref[first_group + steps]
+    begin = bounds_ref[first_group + step]
+    end = bounds_ref[first_group + step + 1]
+
+    def fetch(place):
+        slot = lax.rem(place, DEPTH)
+        block = order_ref[place]
+        return (
+            pltpu.make_async_copy(kernels_ref.at[block], kernel_buf.at[slot], kernel_sem.at[slot]),
+            pltpu.make_async_copy(samples_ref.at[block], sample_buf.at[slot], sample_sem.at[slot]),
+        )
+
+    def start(place):
+        @pl.when(place < last)
+        def _():
+            for copy in fetch(place):
+                copy.start()
+
+    @pl.when(step == 0)
+    def _():
+        for ahead in range(DEPTH):
+            start(first + ahead)
+
+    cosine = cos_ref[...]
+    sine = sin_ref[...]
+    length = spec_ref.shape[0] * spec_ref.shape[2]
+    parts = [
+        jnp.concatenate([spec_ref[:, 2 * col + part].reshape(length, NZ) for col in range(2)], 1)
+        for part in range(2)
+    ]
+    grid_real = (mxu(cosine, parts[0]) + mxu(sine, parts[1])).astype(jnp.bfloat16)
+    grid_imag = (mxu(cosine, parts[1]) - mxu(sine, parts[0])).astype(jnp.bfloat16)
+    per_col = NL // TILE
+    for col in range(2):
+        lanes = slice(col * NZ, (col + 1) * NZ)
+        for tile in range(per_col):
+            cells = slice(tile * TILE, (tile + 1) * TILE)
+            tiles[col * per_col + tile, :, :NZ] = grid_real[cells, lanes]
+            tiles[col * per_col + tile, :, NZ:] = grid_imag[cells, lanes]
+    sums[...] = jnp.zeros_like(sums)
+
+    def one(place, buf):
+        slot = lax.rem(place, DEPTH)
+        tile = local_ref[place]
+        weights = kernel_buf[slot]
+        predicted = mxu(weights, tiles[tile])
+        sample_scr[buf] = sample_buf[slot].astype(jnp.float32)
+        measured = jnp.concatenate(
+            [sample_scr[buf, pl.ds(0, TILE, 2), :], sample_scr[buf, pl.ds(1, TILE, 2), :]], 1
+        )
+        misfit = (predicted - measured).astype(jnp.bfloat16)
+        back = lax.dot_general(
+            weights, misfit, (((0,), (0,)), ((), ())), preferred_element_type=jnp.float32
+        )
+        return tile, back
+
+    def two(pair, carry):
+        place = begin + 2 * pair
+        other = jnp.minimum(place + 1, end - 1)
+        for copy in fetch(place):
+            copy.wait()
+
+        @pl.when(place + 1 < end)
+        def _():
+            for copy in fetch(place + 1):
+                copy.wait()
+
+        tile_a, back_a = one(place, 0)
+        tile_b, back_b = one(other, 1)
+        sums[tile_a] += back_a
+        sums[tile_b] += jnp.where(place + 1 < end, back_b, 0.0)
+        start(place + DEPTH)
+
+        @pl.when(place + 1 < end)
+        def _():
+            start(place + 1 + DEPTH)
+
+        return carry
+
+    lax.fori_loop(0, (end - begin + 1) // 2, two, 0)
+
+    for col in range(2):
+        lanes = slice(col * NZ, (col + 1) * NZ)
+        for tile in range(per_col):
+            cells = slice(tile * TILE, (tile + 1) * TILE)
+            value = sums[col * per_col + tile].astype(jnp.bfloat16)
+            backs[0, cells, lanes] = value[:, :NZ]
+            backs[1, cells, lanes] = value[:, NZ:]
+    back_real = backs[0]
+    back_imag = backs[1]
+    rows_real = mxu(cosine, back_real) - mxu(sine, back_imag)
+    rows_imag = mxu(sine, back_real) + mxu(cosine, back_imag)
+    for col in range(2):
+        lanes = slice(col * NZ, (col + 1) * NZ)
+        base = pl.multiple_of((2 * step + col) * 2 * NL, 2 * NL)
+        moved[pl.ds(base, NL), :] = rows_real[:, lanes]
+        moved[pl.ds(base + NL, NL), :] = rows_imag[:, lanes]
+
+    @pl.when(step == steps - 1)
+    def _():
+        owners, own_rows = spec_ref.shape[0], spec_ref.shape[2]
+        each = own_rows // row_chunks
+        groups = moved.shape[0] // (16 * NL)
+        for piece in range(row_chunks):
+
+            def move(row, carry):
+                owner = row // each
+                source = owner * own_rows + piece * each + lax.rem(row, each)
+                for part in range(2):
+                    start_row = part * NL + source
+                    outs[piece][2 * row + part] = jnp.concatenate(
+                        [
+                            moved[pl.ds(start_row + 16 * NL * group, 8, 2 * NL), :]
+                            for group in range(groups)
+                        ],
+                        0,
+                    ).astype(jnp.bfloat16)
+                return carry
+
+            lax.fori_loop(0, owners * each, move, 0, unroll=4)
+
+
+def column_stage(spectra, tables, kernels, samples, plan, chunk, chunks, row_chunks):
+    owners, width, own_rows = spectra.shape[:3]
+    steps = width // 4
+    per_col = NL // TILE
+    cols = width // 2
+    each = own_rows // row_chunks
+    whole = lambda i, *refs: (0, 0)
+    return pl.pallas_call(
+        functools.partial(columns_kernel, chunk * steps),
+        grid_spec=pltpu.PrefetchScalarGridSpec(
+            num_scalar_prefetch=3,
+            grid=(steps,),
+            in_specs=[
+                pl.BlockSpec((owners, 4, own_rows, NZ), lambda i, *refs: (0, i, 0, 0)),
+                pl.BlockSpec((NL, NL), whole),
+                pl.BlockSpec((NL, NL), whole),
+                pl.BlockSpec(memory_space=pl.ANY),
+                pl.BlockSpec(memory_space=pl.ANY),
+            ],
+            out_specs=[
+                pl.BlockSpec((owners * each * 2, cols, NZ), lambda i, *refs: (0, 0, 0))
+                for _ in range(row_chunks)
+            ],
+            scratch_shapes=[
+                pltpu.VMEM((2 * per_col, TILE, 2 * NZ), jnp.bfloat16),
+                pltpu.VMEM((2 * per_col, TILE, 2 * NZ), jnp.float32),
+                pltpu.VMEM((2, NL, 2 * NZ), jnp.bfloat16),
+                pltpu.VMEM((2, 2 * TILE, NZ), jnp.float32),
+                pltpu.VMEM((cols * 2 * NL, NZ), jnp.float32),
+                pltpu.VMEM((DEPTH, TILE, TILE), jnp.bfloat16),
+                pltpu.VMEM((DEPTH, 2 * TILE, NZ), jnp.bfloat16),
+                pltpu.SemaphoreType.DMA((DEPTH,)),
+                pltpu.SemaphoreType.DMA((DEPTH,)),
+                pltpu.VMEM((8, NZ), jnp.float32),
+            ],
+        ),
+        out_shape=[
+            jax.ShapeDtypeStruct((owners * each * 2, cols, NZ), jnp.bfloat16)
+            for _ in range(row_chunks)
+        ],
+        cost_estimate=pl.CostEstimate(
+            flops=60000000000 // chunks, bytes_accessed=40000000 // chunks, transcendentals=0
+        ),
+    )(*plan, spectra, *tables, kernels, samples)
+
+
+def image_kernel(coil_ref, early_ref, late_ref, maps_ref, cos_ref, sin_ref, own_ref, send_ref, map_scr):
+    coil_id = coil_ref[0]
+    cosine = cos_ref[...]
+    sine = sin_ref[...]
+    count = early_ref.shape[0] * early_ref.shape[3]
+    half = NL // 2
+    parts = []
+    for part in range(2):
+        lanes = []
+        for row in range(2):
+            lanes.append(
+                jnp.concatenate(
+                    [
+                        early_ref[:, row, part].reshape(count, NZ),
+                        late_ref[:, row, part].reshape(count, NZ),
+                    ],
+                    0,
+                )
+            )
+        parts.append(jnp.concatenate(lanes, 1))
+    back_real = mxu(cosine, parts[0]) - mxu(sine, parts[1])
+    back_imag = mxu(sine, parts[0]) + mxu(cosine, parts[1])
+    for row in range(2):
+        lanes = slice(row * NZ, (row + 1) * NZ)
+        for which in range(2):
+            rows = slice(which * half, (which + 1) * half)
+            side = coil_id if which == 0 else 1 - coil_id
+            map_scr[2 * row + which] = maps_ref[row, side].astype(jnp.float32)
+            map_real = map_scr[2 * row + which, pl.ds(0, half, 2), :]
+            map_imag = map_scr[2 * row + which, pl.ds(1, half, 2), :]
+            real = back_real[rows, lanes]
+            imag = back_imag[rows, lanes]
+            term_real = map_real * real + map_imag * imag
+            term_imag = map_real * imag - map_imag * real
+            if which == 0:
+                own_ref[row, 0] = term_real
+                own_ref[row, 1] = term_imag
+            else:
+                send_ref[row, 0] = term_real.astype(jnp.bfloat16)
+                send_ref[row, 1] = term_imag.astype(jnp.bfloat16)
+
+
+def image_stage(coil_id, early, late, maps, tables, piece):
+    owners, each, _, cols = late.shape[:4]
+    half = NL // 2
+    base = piece * each // 2
+    whole = lambda i, *refs: (0, 0)
+    return pl.pallas_call(
+        image_kernel,
+        grid_spec=pltpu.PrefetchScalarGridSpec(
+            num_scalar_prefetch=1,
+            grid=(each // 2,),
+            in_specs=[
+                pl.BlockSpec((owners, 2, 2, cols, NZ), lambda i, *refs: (0, base + i, 0, 0, 0)),
+                pl.BlockSpec((owners, 2, 2, cols, NZ), lambda i, *refs: (0, i, 0, 0, 0)),
+                pl.BlockSpec((2, 2, NL, NZ), lambda i, *refs: (base + i, 0, 0, 0)),
+                pl.BlockSpec((NL, NL), whole),
+                pl.BlockSpec((NL, NL), whole),
+            ],
+            out_specs=[
+                pl.BlockSpec((2, 2, half, NZ), lambda i, *refs: (i, 0, 0, 0)),
+                pl.BlockSpec((2, 2, half, NZ), lambda i, *refs: (i, 0, 0, 0)),
+            ],
+            scratch_shapes=[pltpu.VMEM((4, NL, NZ), jnp.float32)],
+        ),
+        out_shape=[
+            jax.ShapeDtypeStruct((each, 2, half, NZ), jnp.float32),
+            jax.ShapeDtypeStruct((each, 2, half, NZ), jnp.bfloat16),
+        ],
+        cost_estimate=pl.CostEstimate(
+            flops=8 * each * NL * NL * NZ, bytes_accessed=each * 1200000, transcendentals=0
+        ),
+    )(coil_id, early, late, maps, *tables)
+
+
+def sum_kernel(total_ref, own_ref, other_ref, out_ref):
+    half = own_ref.shape[2]
+    for row in range(own_ref.shape[0]):
+        for part in range(2):
+            rows = pl.ds(part, half, 2)
+            out_ref[row, rows, :] = (
+                total_ref[row, rows, :] + own_ref[row, part] + other_ref[row, part].astype(jnp.float32)
+            )
+
+
+def sum_stage(total, own, other, piece):
+    each, _, half = own.shape[:3]
+    rows = 4
+    base = piece * each // rows
+    return pl.pallas_call(
+        sum_kernel,
+        grid=(each // rows,),
+        in_specs=[
+            pl.BlockSpec((rows, 2 * half, NZ), lambda i: (base + i, 0, 0)),
+            pl.BlockSpec((rows, 2, half, NZ), lambda i: (i, 0, 0, 0)),
+            pl.BlockSpec((rows, 2, half, NZ), lambda i: (i, 0, 0, 0)),
+        ],
+        out_specs=pl.BlockSpec((rows, 2 * half, NZ), lambda i: (base + i, 0, 0)),
+        out_shape=jax.ShapeDtypeStruct(total.shape, jnp.float32),
+        input_output_aliases={0: 0},
+        cost_estimate=pl.CostEstimate(
+            flops=4 * each * half * NZ, bytes_accessed=each * 1000000, transcendentals=0
+        ),
+    )(total, own, other)
+
+
+def block_plan(tile_of_block, pen_id, tile_count, group):
+    count = tile_of_block.shape[0]
+    local = tile_of_block - pen_id * tile_count
+    spot = jnp.arange(count, dtype=jnp.int32)
+    key = local * count + spot
+    rank = jnp.sum((key[None, :] < key[:, None]).astype(jnp.int32), 1)
+    hit = (rank[None, :] == spot[:, None]).astype(jnp.int32)
+    order = jnp.sum(hit * spot[None, :], 1)
+    sorted_tile = jnp.sum(hit * local[None, :], 1)
+    edges = jnp.arange(tile_count // group + 1, dtype=jnp.int32) * group
+    bounds = jnp.sum((local[None, :] < edges[:, None]).astype(jnp.int32), 1)
+    return (order, sorted_tile % group, bounds)
+
+
+def on_device_fast(*args):
+    return gradient_parts(*args)
+
+
+def gradient_parts(image_field, coil_maps, samples, kernels, tile_of_block):
+    own_rows = image_field.shape[0]
+    pen_count = lax.axis_size("pen")
+    local_cols = NL // pen_count
+    pen_id = lax.axis_index("pen")
+    coil_id = lax.axis_index("coil")
+    chunks, row_chunks = 2, 4
+    chunk_cols = local_cols // chunks
+    image = image_field.reshape(own_rows, 2 * NL, NZ)
+    maps = coil_maps.reshape(own_rows, 2 * NL, NZ)
+    block_count = kernels.shape[0]
+    sample_rows = samples.reshape(block_count, 2 * TILE, NZ)
+    natural = numpy.arange(NL)
+    split = (
+        natural.reshape(pen_count, chunks, chunk_cols).transpose(1, 0, 2).reshape(NL)
+    )
+    tables_rows = pair_tables(1.0 / 16, split, natural)
+    tables_cols = pair_tables(1.0 / 32, natural, natural)
+    tables_back = pair_tables(1.0 / 16, natural, split)
+    tables_back = [jnp.roll(table, -coil_id * (NL // 2), 0) for table in tables_back]
+    per_col = NL // TILE
+    plan = block_plan(tile_of_block, pen_id, block_count // 2, 2 * per_col)
+
+    def exchange(array):
+        return lax.all_to_all(array, "pen", split_axis=0, concat_axis=0, tiled=True)
+
+    above = shifted(image[-1:], "pen", 1)
+    below = shifted(image[:1], "pen", -1)
+    arrived = []
+    for chunk in range(chunks):
+        spectra = row_spectra(image, maps, tables_rows, chunk, chunks)
+        spectra = spectra.reshape(pen_count, 2 * chunk_cols, own_rows, NZ)
+        arrived.append(exchange(spectra))
+    back = []
+    for chunk in range(chunks):
+        pieces = 1 if chunk == 0 else row_chunks
+        result = column_stage(
+            arrived[chunk], tables_cols, kernels, sample_rows, plan, chunk, chunks, pieces
+        )
+        got = []
+        for piece in range(pieces):
+            one = result[piece].reshape(pen_count, own_rows // pieces, 2, chunk_cols, NZ)
+            got.append(exchange(one))
+        back.append(got)
+    total = variation_stage(image, above, below, jnp.stack([coil_id, pen_id]).astype(jnp.int32))
+    side_maps = maps.reshape(own_rows, 2, NL, NZ)
+    coil_vec = coil_id.reshape(1).astype(jnp.int32)
+    for piece in range(row_chunks):
+        own, send = image_stage(
+            coil_vec, back[0][0], back[1][piece], side_maps, tables_back, piece
+        )
+        other = lax.ppermute(send, "coil", [(0, 1), (1, 0)])
+        total = sum_stage(total, own, other, piece)
+    return total.reshape(own_rows, NL // 2, 2, NZ)
+
+
+def variation_kernel(where_ref, rows_ref, after_ref, above_ref, below_ref, out_ref, window, flux_y, flux_x):
+    coil_id = where_ref[0]
+    pen_id = where_ref[1]
+    step = pl.program_id(0)
+    steps = pl.num_programs(0)
+    count = rows_ref.shape[0]
+    half = out_ref.shape[1]
+    offset = pl.multiple_of(coil_id * half, half)
+    before = pl.multiple_of(jnp.maximum(offset - 8, 0), 8)
+    behind = pl.multiple_of(jnp.minimum(offset + half, 2 * NL - 8), 8)
+    lane = lax.broadcasted_iota(jnp.int32, (1, NZ), 1)
+    not_last_plane = (lane != NZ - 1).astype(jnp.float32)
+
+    def place(slot, ref, row):
+        window[slot, pl.ds(0, 8), :] = ref[row, pl.ds(before, 8), :]
+        window[slot, pl.ds(8, half), :] = ref[row, pl.ds(offset, half), :]
+        window[slot, pl.ds(half + 8, 8), :] = ref[row, pl.ds(behind, 8), :]
+
+    def flux(slot, next_slot, start, size, row_scale):
+        center = window[slot, pl.ds(start, size), :]
+        row = lax.broadcasted_iota(jnp.int32, (size, NZ), 0)
+        column_row = row + (start - 8) + offset
+        not_last = jnp.where(column_row < 2 * NL - 2, 1.0, 0.0)
+        diff_y = (window[next_slot, pl.ds(start, size), :] - center) * row_scale
+        diff_x = (window[slot, pl.ds(start + 2, size), :] - center) * not_last
+        diff_z = (pltpu.roll(center, NZ - 1, 1) - center) * not_last_plane
+        square = diff_y * diff_y + diff_x * diff_x + diff_z * diff_z
+        split = square.reshape(size // 8, 8, NZ)
+        up = pltpu.roll(split, 7, 1).reshape(size, NZ)
+        down = pltpu.roll(split, 1, 1).reshape(size, NZ)
+        square = square + jnp.where(row % 2 == 0, up, down)
+        scale = lax.rsqrt(1.0 + square)
+        return diff_y * scale, diff_x * scale, diff_z * scale
+
+    size = half // 4
+
+    @pl.when(step == 0)
+    def _():
+        place(1, above_ref, 0)
+        place(0, rows_ref, 0)
+        inside = jnp.where(pen_id > 0, 1.0, 0.0)
+
+        def first(part, carry):
+            start = pl.multiple_of(8 + part * size, 8)
+            flux_y[pl.ds(start - 8, size), :] = flux(1, 0, start, size, 1.0)[0] * inside
+            return carry
+
+        lax.fori_loop(0, 4, first, 0)
+
+    last_step = step == steps - 1
+    last_pen = pen_id == lax.axis_size("pen") - 1
+
+    def one_row(row, carry):
+        slot = lax.rem(row, 2)
+        is_end = row == count - 1
+
+        @pl.when(jnp.logical_not(is_end))
+        def _():
+            place(1 - slot, rows_ref, jnp.minimum(row + 1, count - 1))
+
+        @pl.when(jnp.logical_and(is_end, jnp.logical_not(last_step)))
+        def _():
+            place(1 - slot, after_ref, 0)
+
+        @pl.when(jnp.logical_and(is_end, last_step))
+        def _():
+            place(1 - slot, below_ref, 0)
+
+        row_scale = jnp.where(
+            jnp.logical_and(jnp.logical_and(is_end, last_step), last_pen), 0.0, 1.0
+        )
+        edge = flux(slot, 1 - slot, 0, 8, row_scale)[1]
+        flux_x[pl.ds(0, 8), :] = edge * jnp.where(coil_id > 0, 1.0, 0.0)
+
+        def part_of(part, carry):
+            start = pl.multiple_of(8 + part * size, 8)
+            here_y, here_x, here_z = flux(slot, 1 - slot, start, size, row_scale)
+            flux_x[pl.ds(start, size), :] = here_x
+            past_y = flux_y[pl.ds(start - 8, size), :]
+            flux_y[pl.ds(start - 8, size), :] = here_y
+            past_x = flux_x[pl.ds(start - 2, size), :]
+            past_z = pltpu.roll(here_z, 1, 1)
+            total = (past_y - here_y) + (past_x - here_x) + (past_z - here_z)
+            out_ref[row, pl.ds(start - 8, size), :] = tv_weight * total
+            return carry
+
+        lax.fori_loop(0, 4, part_of, 0)
+        return carry
+
+    lax.fori_loop(0, count, one_row, 0)
+
+
+def variation_stage(image, above, below, where):
+    rows = image.shape[0]
+    count = 8
+    return pl.pallas_call(
+        variation_kernel,
+        grid_spec=pltpu.PrefetchScalarGridSpec(
+            num_scalar_prefetch=1,
+            grid=(rows // count,),
+            in_specs=[
+                pl.BlockSpec((count, 2 * NL, NZ), lambda i, *refs: (i, 0, 0)),
+                pl.BlockSpec(
+                    (1, 2 * NL, NZ), lambda i, *refs: (jnp.minimum(count * (i + 1), rows - 1), 0, 0)
+                ),
+                pl.BlockSpec((1, 2 * NL, NZ), lambda i, *refs: (0, 0, 0)),
+                pl.BlockSpec((1, 2 * NL, NZ), lambda i, *refs: (0, 0, 0)),
+            ],
+            out_specs=pl.BlockSpec((count, NL, NZ), lambda i, *refs: (i, 0, 0)),
+            scratch_shapes=[
+                pltpu.VMEM((2, NL + 16, NZ), jnp.float32),
+                pltpu.VMEM((NL, NZ), jnp.float32),
+                pltpu.VMEM((NL + 8, NZ), jnp.float32),
+            ],
+        ),
+        out_shape=jax.ShapeDtypeStruct((rows, NL, NZ), jnp.float32),
+        cost_estimate=pl.CostEstimate(
+            flops=40 * rows * NL * NZ, bytes_accessed=60000000, transcendentals=0
+        ),
+        name="variation",
+    )(where, image, image, above, below)
+
+
 def solution(mesh):
     in_specs = (
         P("pen", None, None, None),
@@ -154,6 +731,8 @@
         P("pen"),
     )
     out_specs = P("pen", "coil", None, None)
+    own_rows = NL // mesh.shape["pen"]
+    body = on_device_fast if own_rows % 32 == 0 else on_device
     return jax.shard_map(
-        on_device, mesh=mesh, in_specs=in_specs, out_specs=out_specs, check_vma=False
-    )
+        body, mesh=mesh, in_specs=in_specs, out_specs=out_specs, check_vma=False
+    )

time: 1360 us -> 547 us (0.40)
  local copies, waits for them, and re-layouts: 393 us -> 8.25 us
  waiting for transfers between devices: 356 us -> 107 us
  Pallas kernels: 0 us -> 210 us
  matrix products: 189 us -> 0 us
  other arithmetic: 169 us -> 2.84 us
  blocking collectives: 219 us -> 172 us
  starting transfers between devices: 10.4 us -> 46 us
  between operations: 14.1 us -> 0.13 us
    psum x1 -> x0, waiting for transfers between devices: 251 us -> none  [on_device(): summed = lax.psum(coil_term, 'coil')]
    pallas_call x0 -> x13, Pallas kernels: none -> 210 us  [the longest x2 102 us: column_stage(): pl.pallas_call(functools.partial(columns_kernel, chunk * steps), grid_spe...]
    dot_general x10 -> x0, matrix products: 189 us -> none  [the longest x1 38.4 us: on_device(): jnp.einsum('bst,bsc->btc', kernels, misfit, preferred_element_type=jnp.fl...]
    convert_element_type x3 -> x0, local copies, waits for them, and re-layouts: 87.6 us -> none  [the longest x1 45.1 us: on_device(): measured = samples[0].reshape(predicted.shape).astype(jnp.float32)]
    unnamed x29 -> x14, local copies, waits for them, and re-layouts: 64.2 us -> 3.91 us
    all_to_all x5 -> x0, local copies, waits for them, and re-layouts: 57.7 us -> none  [the longest x3 39.8 us: on_device(): lax.all_to_all(rows_spectrum, 'pen', split_axis=1, concat_axis=0, tiled=T...]
    reshape x4 -> x0, local copies, waits for them, and re-layouts: 51.6 us -> none  [the longest x2 25.8 us: on_device(): kspace_grid.reshape(NL // TILE, TILE, local_cols, 2 * NZ)]
    all_to_all x1 -> x3, blocking collectives: 219 us -> 172 us  [exchange(): return lax.all_to_all(array, 'pen', split_axis=0, concat_axis=0, tiled=True)]
  transfers between devices with their start and end apart: 4 -> 10, of which waited for: 2 -> 5; matrix products, arithmetic and copies ran while one was open for 13% -> 1% of each run, Pallas kernels for 0% -> 35%
where the time goes in v1:
time: 547 us; the launch traced here: 546 us
  Pallas kernels  210 us (38%)
  blocking collectives  172 us (31%)
  waiting for transfers between devices  107 us (20%)
  starting transfers between devices  46 us (8%)
  local copies, waits for them, and re-layouts  8.25 us (2%)
    all_to_all x3, blocking collectives, exchange(): return lax.all_to_all(array, 'pen', split_axis=0, concat_axis=0, tiled=True)  172 us
    pallas_call x2, Pallas kernels, column_stage(): pl.pallas_call(functools.partial(columns_kernel, chunk * steps), grid_spe...  102 us
    all_to_all x4, waiting for transfers between devices, exchange(): return lax.all_to_all(array, 'pen', split_axis=0, concat_axis=0, tiled=True)  84.3 us
    all_to_all x4, starting transfers between devices, exchange(): return lax.all_to_all(array, 'pen', split_axis=0, concat_axis=0, tiled=True)  37.5 us
    pallas_call x2, Pallas kernels, row_spectra(): pl.pallas_call(rows_kernel, grid=(rows // 16, 2), in_specs=[pl.BlockSpec(...  35.9 us
    pallas_call x1, Pallas kernels, variation_stage(): pl.pallas_call(variation_kernel, grid_spec=pltpu.PrefetchScalarGridSpec(n...  33.1 us
    pallas_call x4, Pallas kernels, image_stage(): pl.pallas_call(image_kernel, grid_spec=pltpu.PrefetchScalarGridSpec(num_s...  24.4 us
    ppermute x4, waiting for transfers between devices, gradient_parts(): other = lax.ppermute(send, 'coil', [(0, 1), (1, 0)])  20.3 us
  transfers between devices with their start and end apart: 10, of which 5 were waited for; matrix products, arithmetic and copies ran while one was open for 1% of the time, Pallas kernels for 35%

profile of v1, /device:TPU:0, one launch (start us, length us, event | category | flops | bytes accessed | tf_op | source)
XLA Modules:
  0.0 545.9 jit_solution(2138732898655326372)
XLA Ops:
  0.0 17.9 %shard_map.111 = bf16[512,32,128]{2,1,0:T(8,128)(2,1)} custom-call(f32[32,1024,128]{2,1,0:T(8,128)} %bitcast.22, bf16[32,1024,128]{2,1,0:T(8,128)(2,1)} %bitcast.16, bf16[512,512]{1,0:T(8,128)(2,1)} %constant.61.clone.cos_ref, bf16[512,512]{1,0:T(8,128)(2,1)} %constant.62.clone.sin_ref), custom_call_target="tpu_custom_call" | custom-call | flops 4294967296 | bytes 30000000 | tf_op jit(solution)/shard_map/pallas_call | solution.py:210
  17.9 7.4 %all-to-all-start.2 = ((bf16[16,32,32,128]{3,2,1,0:T(8,128)(2,1)}), bf16[16,32,32,128]{3,2,1,0:T(8,128)(2,1)}, u32[]{:S(2)}, u32[]{:S(2)}) async-start(bf16[16,32,32,128]{3,2,1,0:T(8,128)(2,1)} %bitcast.27), calls=%async_computation.2 | async-start | bytes 8388608 | tf_op jit(solution)/shard_map/all_to_all | solution.py:570
  25.4 17.9 %shard_map.109 = bf16[512,32,128]{2,1,0:T(8,128)(2,1)} custom-call(f32[32,1024,128]{2,1,0:T(8,128)} %bitcast.23, bf16[32,1024,128]{2,1,0:T(8,128)(2,1)} %bitcast.17, bf16[512,512]{1,0:T(8,128)(2,1)} %constant.61.clone.cos_ref, bf16[512,512]{1,0:T(8,128)(2,1)} %constant.62.clone.sin_ref), custom_call_target="tpu_custom_call" | custom-call | flops 4294967296 | bytes 30000000 | tf_op jit(solution)/shard_map/pallas_call | solution.py:210
  43.3 59.6 %all-to-all-done.2.spec_ref = bf16[16,32,32,128]{3,2,1,0:T(8,128)(2,1)} async-done(((bf16[16,32,32,128]{3,2,1,0:T(8,128)(2,1)}), bf16[16,32,32,128]{3,2,1,0:T(8,128)(2,1)}, u32[]{:S(2)}, u32[]{:S(2)}) %all-to-all-start.2) | async-done | bytes 4194336 | tf_op jit(solution)/shard_map/all_to_all | solution.py:570
  102.9 19.7 %all-to-all-start = ((bf16[16,32,32,128]{3,2,1,0:T(8,128)(2,1)}), bf16[16,32,32,128]{3,2,1,0:T(8,128)(2,1)}, u32[]{:S(2)}, u32[]{:S(2)}) async-start(bf16[16,32,32,128]{3,2,1,0:T(8,128)(2,1)} %bitcast.26), calls=%async_computation | async-start | bytes 8388608 | tf_op jit(solution)/shard_map/all_to_all | solution.py:570
  124.8 50.6 %shard_map.112 = (bf16[256,16,128]{2,1,0:T(8,128)(2,1)}, bf16[256,16,128]{2,1,0:T(8,128)(2,1)}, bf16[256,16,128]{2,1,0:T(8,128)(2,1)}, bf16[256,16,128]{2,1,0:T(8,128)(2,1)}) custom-call(s32[256]{0:T(256)} %get-tuple-element.31.order_ref, s32[256]{0:T(256)} %and_select_fusion.local_ref, s32[17]{0:T(128)} %convert_reduce_fusion.1.bounds_ref, ...), custom_call_target="tpu_custom_call" | custom-call | flops 30000001024 | bytes 20000000 | tf_op jit(solution)/shard_map/pallas_call | solution.py:383
  175.5 24.7 %all-to-all-done.spec_ref = bf16[16,32,32,128]{3,2,1,0:T(8,128)(2,1)} async-done(((bf16[16,32,32,128]{3,2,1,0:T(8,128)(2,1)}), bf16[16,32,32,128]{3,2,1,0:T(8,128)(2,1)}, u32[]{:S(2)}, u32[]{:S(2)}) %all-to-all-start) | async-done | bytes 4194336 | tf_op jit(solution)/shard_map/all_to_all | solution.py:570
  200.2 44.4 %all_to_all.35.late_ref = bf16[16,8,2,16,128]{4,3,2,1,0:T(8,128)(2,1)} all-to-all(bf16[16,8,2,16,128]{4,3,2,1,0:T(8,128)(2,1)} %bitcast.31), channel_id=1, replica_groups=mesh['pen'=16,'coil'=2] {'pen'}, dimensions={0} | all-to-all | bytes 2097152 | tf_op jit(solution)/shard_map/all_to_all | solution.py:570
  244.6 29.8 %all_to_all.36.late_ref = bf16[16,8,2,16,128]{4,3,2,1,0:T(8,128)(2,1)} all-to-all(bf16[16,8,2,16,128]{4,3,2,1,0:T(8,128)(2,1)} %bitcast.30), channel_id=1, replica_groups=mesh['pen'=16,'coil'=2] {'pen'}, dimensions={0} | all-to-all | bytes 2097152 | tf_op jit(solution)/shard_map/all_to_all | solution.py:570
  274.4 5.0 all-to-all-start.5
  279.5 51.7 %shard_map.110 = bf16[1024,16,128]{2,1,0:T(8,128)(2,1)} custom-call(s32[256]{0:T(256)} %get-tuple-element.31.order_ref, s32[256]{0:T(256)} %and_select_fusion.local_ref, s32[17]{0:T(128)} %convert_reduce_fusion.1.bounds_ref, bf16[16,32,32,128]{3,2,1,0:T(8,128)(2,1)} %all-to-all-done.spec_ref, bf16[512,512]{1,0:T(8,128)(2,1)} %constant.63.clone.cos_ref, ...), custom_call_target="tpu_custom_call" | custom-call | flops 30000001024 | bytes 20000000 | tf_op jit(solution)/shard_map/pallas_call | solution.py:383
  331.2 97.7 %all_to_all.37.early_ref = bf16[16,32,2,16,128]{4,3,2,1,0:T(8,128)(2,1)} all-to-all(bf16[16,32,2,16,128]{4,3,2,1,0:T(8,128)(2,1)} %bitcast.28), channel_id=1, replica_groups=mesh['pen'=16,'coil'=2] {'pen'}, dimensions={0} | all-to-all | bytes 8388608 | tf_op jit(solution)/shard_map/all_to_all | solution.py:570
  428.9 5.3 all-to-all-start.6
  434.3 2.3 fusion.1
  436.5 3.1 collective-permute-start
  439.6 2.1 constant_dynamic-slice_fusion
  441.7 6.0 %shard_map.113 = (f32[8,2,256,128]{3,2,1,0:T(8,128)}, bf16[8,2,256,128]{3,2,1,0:T(8,128)(2,1)}) custom-call(s32[1]{0:T(128)} %bitcast.coil_ref, bf16[16,32,2,16,128]{4,3,2,1,0:T(8,128)(2,1)} %all_to_all.37.early_ref, bf16[16,8,2,16,128]{4,3,2,1,0:T(8,128)(2,1)} %all_to_all.35.late_ref, bf16[32,2,512,128]{3,2,1,0:T(8,128)(2,1)} %bitcast.18, ...), custom_call_target="tpu_custom_call" | custom-call | flops 2147483648 | bytes 9600000 | tf_op jit(solution)/shard_map/pallas_call | solution.py:469
  447.8 1.6 collective-permute-start.2
  449.3 6.1 %shard_map.115 = (f32[8,2,256,128]{3,2,1,0:T(8,128)}, bf16[8,2,256,128]{3,2,1,0:T(8,128)(2,1)}) custom-call(s32[1]{0:T(128)} %bitcast.coil_ref, bf16[16,32,2,16,128]{4,3,2,1,0:T(8,128)(2,1)} %all_to_all.37.early_ref, bf16[16,8,2,16,128]{4,3,2,1,0:T(8,128)(2,1)} %all_to_all.36.late_ref, bf16[32,2,512,128]{3,2,1,0:T(8,128)(2,1)} %bitcast.19, ...), custom_call_target="tpu_custom_call" | custom-call | flops 2147483648 | bytes 9600000 | tf_op jit(solution)/shard_map/pallas_call | solution.py:469
  455.9 6.1 %shard_map.117 = (f32[8,2,256,128]{3,2,1,0:T(8,128)}, bf16[8,2,256,128]{3,2,1,0:T(8,128)(2,1)}) custom-call(s32[1]{0:T(128)} %bitcast.coil_ref, bf16[16,32,2,16,128]{4,3,2,1,0:T(8,128)(2,1)} %all_to_all.37.early_ref, bf16[16,8,2,16,128]{4,3,2,1,0:T(8,128)(2,1)} %copy-done, bf16[32,2,512,128]{3,2,1,0:T(8,128)(2,1)} %bitcast.20, ...), custom_call_target="tpu_custom_call" | custom-call | flops 2147483648 | bytes 9600000 | tf_op jit(solution)/shard_map/pallas_call | solution.py:469
  462.0 1.5 collective-permute-start.4
  464.5 6.1 %shard_map.119 = (f32[8,2,256,128]{3,2,1,0:T(8,128)}, bf16[8,2,256,128]{3,2,1,0:T(8,128)(2,1)}) custom-call(s32[1]{0:T(128)} %bitcast.coil_ref, bf16[16,32,2,16,128]{4,3,2,1,0:T(8,128)(2,1)} %all_to_all.37.early_ref, bf16[16,8,2,16,128]{4,3,2,1,0:T(8,128)(2,1)} %copy-done.1, bf16[32,2,512,128]{3,2,1,0:T(8,128)(2,1)} %bitcast.21, ...), custom_call_target="tpu_custom_call" | custom-call | flops 2147483648 | bytes 9600000 | tf_op jit(solution)/shard_map/pallas_call | solution.py:469
  471.2 1.3 collective-permute-start.1
  473.1 2.2 collective-permute-done.1.below_ref
  475.3 33.1 %variation.1.total_ref = f32[32,512,128]{2,1,0:T(8,128)} custom-call(s32[2]{0:T(128)} %pad_add_fusion.where_ref, f32[32,1024,128]{2,1,0:T(8,128)} %bitcast.24, f32[32,1024,128]{2,1,0:T(8,128)} %bitcast.25, f32[1,1024,128]{2,1,0:T(8,128)} %collective-permute-done.above_ref, f32[1,1024,128]{2,1,0:T(8,128)} %collective-permute-done.1.below_ref), custom_call_target="tpu_custom_call" | custom-call | flops 83886080 | bytes 60000000 | tf_op jit(solution)/shard_map/variation/pallas_call | solution.py:697
  508.4 3.6 shard_map.114.total_ref
  513.0 3.6 shard_map.116.total_ref
  516.6 2.4 collective-permute-done.4.other_ref
  519.0 1.0 copy-done.2
  520.0 3.6 shard_map.118.total_ref
  523.5 17.8 %collective-permute-done.5.other_ref = bf16[8,2,256,128]{3,2,1,0:T(8,128)(2,1)S(1)} collective-permute-done((bf16[8,2,256,128]{3,2,1,0:T(8,128)(2,1)}, bf16[8,2,256,128]{3,2,1,0:T(8,128)(2,1)S(1)}, u32[]{:S(2)}, u32[]{:S(2)}) %collective-permute-start.5) | collective-permute-done | bytes 1048608 | tf_op jit(solution)/shard_map/ppermute | solution.py:597
  542.3 3.6 shard_map.120
  (27 shorter events, 6.8 us)
Async XLA Ops:
  17.9 85.0 %all-to-all-start.2 = ((bf16[16,32,32,128]{3,2,1,0:T(8,128)(2,1)}), bf16[16,32,32,128]{3,2,1,0:T(8,128)(2,1)}, u32[]{:S(2)}, u32[]{:S(2)}) async-start(bf16[16,32,32,128]{3,2,1,0:T(8,128)(2,1)} %bitcast.27), calls=%async_computation.2 | async-start | bytes 8388608 | tf_op jit(solution)/shard_map/all_to_all | solution.py:570
  43.3 79.4 %copy-start.6 = (s32[256]{0:T(256)S(1)}, s32[256]{0:T(256)}, u32[]{:S(2)}) copy-start(s32[256]{0:T(256)} %param.17) | copy-start | bytes 3076
  102.9 97.2 %all-to-all-start = ((bf16[16,32,32,128]{3,2,1,0:T(8,128)(2,1)}), bf16[16,32,32,128]{3,2,1,0:T(8,128)(2,1)}, u32[]{:S(2)}, u32[]{:S(2)}) async-start(bf16[16,32,32,128]{3,2,1,0:T(8,128)(2,1)} %bitcast.26), calls=%async_computation | async-start | bytes 8388608 | tf_op jit(solution)/shard_map/all_to_all | solution.py:570
  274.4 56.8 %all-to-all-start.5 = ((bf16[16,8,2,16,128]{4,3,2,1,0:T(8,128)(2,1)}), bf16[16,8,2,16,128]{4,3,2,1,0:T(8,128)(2,1)S(1)}, u32[]{:S(2)}, u32[]{:S(2)}) async-start(bf16[16,8,2,16,128]{4,3,2,1,0:T(8,128)(2,1)} %bitcast.29), calls=%async_computation.5 | async-start | bytes 2097152 | tf_op jit(solution)/shard_map/all_to_all | solution.py:570
  331.2 108.4 %copy-start.5 = (bf16[1024,512]{1,0:T(8,128)(2,1)S(1)}, bf16[1024,512]{1,0:T(8,128)(2,1)}, u32[]{:S(2)}) copy-start(bf16[1024,512]{1,0:T(8,128)(2,1)} %constant.71) | copy-start | bytes 3145732
  331.2 116.5 %copy-start = (bf16[16,8,2,16,128]{4,3,2,1,0:T(8,128)(2,1)}, bf16[16,8,2,16,128]{4,3,2,1,0:T(8,128)(2,1)S(1)}, u32[]{:S(2)}) copy-start(bf16[16,8,2,16,128]{4,3,2,1,0:T(8,128)(2,1)S(1)} %all-to-all-done.5.late_ref) | copy-start | bytes 3145732
  428.9 34.6 %all-to-all-start.6 = ((bf16[16,8,2,16,128]{4,3,2,1,0:T(8,128)(2,1)}), bf16[16,8,2,16,128]{4,3,2,1,0:T(8,128)(2,1)S(1)}, u32[]{:S(2)}, u32[]{:S(2)}) async-start(bf16[16,8,2,16,128]{4,3,2,1,0:T(8,128)(2,1)} %bitcast.14), calls=%async_computation.6 | async-start | bytes 2097152 | tf_op jit(solution)/shard_map/all_to_all | solution.py:570
  436.5 34.7 %collective-permute-start = (f32[1,1024,128]{2,1,0:T(8,128)}, f32[1,1024,128]{2,1,0:T(8,128)}, u32[]{:S(2)}, u32[]{:S(2)}) collective-permute-start(f32[1,1024,128]{2,1,0:T(8,128)} %bitcast.3), channel_id=1, source_target_pairs={{0,2},{2,4},{4,6},{6,8},{8,10},{10,12},{12,14},{14,16},{16,18},{18... | collective-permute-start | bytes 1572872 | tf_op jit(solution)/shard_map/ppermute | solution.py:25
  447.8 60.7 %collective-permute-start.2 = (bf16[8,2,256,128]{3,2,1,0:T(8,128)(2,1)}, bf16[8,2,256,128]{3,2,1,0:T(8,128)(2,1)}, u32[]{:S(2)}, u32[]{:S(2)}) collective-permute-start(bf16[8,2,256,128]{3,2,1,0:T(8,128)(2,1)} %get-tuple-element.20), channel_id=1, source_target_pairs={{0,1},{1,0},{2,3},{3,2},{4,5},{5,4},{6,7},{7,6},{8,9},{9,8},{10,11... | collective-permute-start | bytes 3145736 | tf_op jit(solution)/shard_map/ppermute | solution.py:597
  455.4 56.6 %collective-permute-start.3 = (bf16[8,2,256,128]{3,2,1,0:T(8,128)(2,1)}, bf16[8,2,256,128]{3,2,1,0:T(8,128)(2,1)S(1)}, u32[]{:S(2)}, u32[]{:S(2)}) collective-permute-start(bf16[8,2,256,128]{3,2,1,0:T(8,128)(2,1)} %get-tuple-element.23), channel_id=1, source_target_pairs={{0,1},{1,0},{2,3},{3,2},{4,5},{5,4},{6,7},{7,6},{8,9},{9,8},{10,11... | collective-permute-start | bytes 3145736 | tf_op jit(solution)/shard_map/ppermute | solution.py:597
  462.0 56.9 %collective-permute-start.4 = (bf16[8,2,256,128]{3,2,1,0:T(8,128)(2,1)}, bf16[8,2,256,128]{3,2,1,0:T(8,128)(2,1)S(1)}, u32[]{:S(2)}, u32[]{:S(2)}) collective-permute-start(bf16[8,2,256,128]{3,2,1,0:T(8,128)(2,1)} %get-tuple-element.26), channel_id=1, source_target_pairs={{0,1},{1,0},{2,3},{3,2},{4,5},{5,4},{6,7},{7,6},{8,9},{9,8},{10,11... | collective-permute-start | bytes 3145736 | tf_op jit(solution)/shard_map/ppermute | solution.py:597
  463.6 1.0 copy-start.1
  470.7 70.7 %collective-permute-start.5 = (bf16[8,2,256,128]{3,2,1,0:T(8,128)(2,1)}, bf16[8,2,256,128]{3,2,1,0:T(8,128)(2,1)S(1)}, u32[]{:S(2)}, u32[]{:S(2)}) collective-permute-start(bf16[8,2,256,128]{3,2,1,0:T(8,128)(2,1)} %get-tuple-element.29), channel_id=1, source_target_pairs={{0,1},{1,0},{2,3},{3,2},{4,5},{5,4},{6,7},{7,6},{8,9},{9,8},{10,11... | collective-permute-start | bytes 3145736 | tf_op jit(solution)/shard_map/ppermute | solution.py:597
  471.2 4.1 collective-permute-start.1
  512.0 1.0 copy-start.3
  519.0 1.0 copy-start.2
  541.4 1.0 copy-start.4

commit v2 on v1

--- a/solution.py
+++ b/solution.py
@@ -233,9 +233,11 @@
 
 def columns_kernel(
     first_group,
+    jobs,
     order_ref,
     local_ref,
     bounds_ref,
+    pen_ref,
     spec_ref,
     cos_ref,
     sin_ref,
@@ -243,10 +245,10 @@
     samples_ref,
     *rest,
 ):
-    row_chunks = len(rest) - 10
-    outs = rest[:row_chunks]
+    out_count = len(jobs)
+    outs = rest[:out_count]
     tiles, sums, backs, sample_scr, moved, kernel_buf, sample_buf, kernel_sem, sample_sem, _ = rest[
-        row_chunks:
+        out_count:
     ]
     step = pl.program_id(0)
     steps = pl.num_programs(0)
@@ -351,17 +353,22 @@
 
     @pl.when(step == steps - 1)
     def _():
-        owners, own_rows = spec_ref.shape[0], spec_ref.shape[2]
-        each = own_rows // row_chunks
+        own_rows = spec_ref.shape[2]
         groups = moved.shape[0] // (16 * NL)
-        for piece in range(row_chunks):
+        for out, (kind, which, count, base_row, each) in zip(outs, jobs):
+            if kind == "cross":
+                base_owner = pen_ref[0] ^ which
+            elif kind == "near":
+                base_owner = pen_ref[0] & which
+            else:
+                base_owner = 0
 
             def move(row, carry):
-                owner = row // each
-                source = owner * own_rows + piece * each + lax.rem(row, each)
+                owner = base_owner + row // each
+                source = owner * own_rows + base_row + lax.rem(row, each)
                 for part in range(2):
                     start_row = part * NL + source
-                    outs[piece][2 * row + part] = jnp.concatenate(
+                    out[2 * row + part] = jnp.concatenate(
                         [
                             moved[pl.ds(start_row + 16 * NL * group, 8, 2 * NL), :]
                             for group in range(groups)
@@ -370,20 +377,19 @@
                     ).astype(jnp.bfloat16)
                 return carry
 
-            lax.fori_loop(0, owners * each, move, 0, unroll=4)
-
-
-def column_stage(spectra, tables, kernels, samples, plan, chunk, chunks, row_chunks):
+            lax.fori_loop(0, count * each, move, 0, unroll=2)
+
+
+def column_stage(spectra, tables, kernels, samples, plan, chunk, chunks, jobs):
     owners, width, own_rows = spectra.shape[:3]
     steps = width // 4
     per_col = NL // TILE
     cols = width // 2
-    each = own_rows // row_chunks
     whole = lambda i, *refs: (0, 0)
     return pl.pallas_call(
-        functools.partial(columns_kernel, chunk * steps),
+        functools.partial(columns_kernel, chunk * steps, jobs),
         grid_spec=pltpu.PrefetchScalarGridSpec(
-            num_scalar_prefetch=3,
+            num_scalar_prefetch=4,
             grid=(steps,),
             in_specs=[
                 pl.BlockSpec((owners, 4, own_rows, NZ), lambda i, *refs: (0, i, 0, 0)),
@@ -393,8 +399,8 @@
                 pl.BlockSpec(memory_space=pl.ANY),
             ],
             out_specs=[
-                pl.BlockSpec((owners * each * 2, cols, NZ), lambda i, *refs: (0, 0, 0))
-                for _ in range(row_chunks)
+                pl.BlockSpec((count * each * 2, cols, NZ), lambda i, *refs: (0, 0, 0))
+                for kind, which, count, base_row, each in jobs
             ],
             scratch_shapes=[
                 pltpu.VMEM((2 * per_col, TILE, 2 * NZ), jnp.bfloat16),
@@ -410,8 +416,8 @@
             ],
         ),
         out_shape=[
-            jax.ShapeDtypeStruct((owners * each * 2, cols, NZ), jnp.bfloat16)
-            for _ in range(row_chunks)
+            jax.ShapeDtypeStruct((count * each * 2, cols, NZ), jnp.bfloat16)
+            for kind, which, count, base_row, each in jobs
         ],
         cost_estimate=pl.CostEstimate(
             flops=60000000000 // chunks, bytes_accessed=40000000 // chunks, transcendentals=0
@@ -419,26 +425,31 @@
     )(*plan, spectra, *tables, kernels, samples)
 
 
-def image_kernel(coil_ref, early_ref, late_ref, maps_ref, cos_ref, sin_ref, own_ref, send_ref, map_scr):
-    coil_id = coil_ref[0]
+def image_kernel(crosses, where_ref, early_ref, near_ref, *rest):
+    cross_refs = rest[: len(crosses)]
+    maps_ref, cos_ref, sin_ref, own_ref, send_ref, map_scr, late = rest[len(crosses) :]
+    coil_id = where_ref[0]
+    pen_id = where_ref[1]
     cosine = cos_ref[...]
     sine = sin_ref[...]
-    count = early_ref.shape[0] * early_ref.shape[3]
+    cols = early_ref.shape[3]
+    count = early_ref.shape[0] * cols
+    near = near_ref.shape[0]
     half = NL // 2
     parts = []
     for part in range(2):
         lanes = []
         for row in range(2):
-            lanes.append(
-                jnp.concatenate(
-                    [
-                        early_ref[:, row, part].reshape(count, NZ),
-                        late_ref[:, row, part].reshape(count, NZ),
-                    ],
-                    0,
-                )
+            spot = slice(row * NZ, (row + 1) * NZ)
+            lanes.append(early_ref[:, row, part].reshape(count, NZ))
+            base = pl.multiple_of((pen_id & near) * cols, cols)
+            late[part, pl.ds(base, near * cols), spot] = near_ref[:, row, part].reshape(
+                near * cols, NZ
             )
-        parts.append(jnp.concatenate(lanes, 1))
+            for which, cross_ref in zip(crosses, cross_refs):
+                base = pl.multiple_of((pen_id ^ which) * cols, cols)
+                late[part, pl.ds(base, cols), spot] = cross_ref[row, part]
+        parts.append(jnp.concatenate([jnp.concatenate(lanes, 1), late[part]], 0))
     back_real = mxu(cosine, parts[0]) - mxu(sine, parts[1])
     back_imag = mxu(sine, parts[0]) + mxu(cosine, parts[1])
     for row in range(2):
@@ -461,19 +472,28 @@
                 send_ref[row, 1] = term_imag.astype(jnp.bfloat16)
 
 
-def image_stage(coil_id, early, late, maps, tables, piece):
-    owners, each, _, cols = late.shape[:4]
+def image_stage(where, early, near, crosses, across, maps, tables, base_row, early_row):
+    each, _, cols = across[0].shape[:3]
+    owners = early.shape[0]
     half = NL // 2
-    base = piece * each // 2
+    base = base_row // 2
+    early_base = early_row // 2
     whole = lambda i, *refs: (0, 0)
     return pl.pallas_call(
-        image_kernel,
+        functools.partial(image_kernel, crosses),
         grid_spec=pltpu.PrefetchScalarGridSpec(
             num_scalar_prefetch=1,
             grid=(each // 2,),
             in_specs=[
-                pl.BlockSpec((owners, 2, 2, cols, NZ), lambda i, *refs: (0, base + i, 0, 0, 0)),
-                pl.BlockSpec((owners, 2, 2, cols, NZ), lambda i, *refs: (0, i, 0, 0, 0)),
+                pl.BlockSpec(
+                    (owners, 2, 2, cols, NZ), lambda i, *refs: (0, early_base + i, 0, 0, 0)
+                ),
+                pl.BlockSpec(
+                    (near.shape[0], 2, 2, cols, NZ), lambda i, *refs: (0, base + i, 0, 0, 0)
+                ),
+            ]
+            + [pl.BlockSpec((2, 2, cols, NZ), lambda i, *refs: (i, 0, 0, 0)) for one in across]
+            + [
                 pl.BlockSpec((2, 2, NL, NZ), lambda i, *refs: (base + i, 0, 0, 0)),
                 pl.BlockSpec((NL, NL), whole),
                 pl.BlockSpec((NL, NL), whole),
@@ -482,7 +502,10 @@
                 pl.BlockSpec((2, 2, half, NZ), lambda i, *refs: (i, 0, 0, 0)),
                 pl.BlockSpec((2, 2, half, NZ), lambda i, *refs: (i, 0, 0, 0)),
             ],
-            scratch_shapes=[pltpu.VMEM((4, NL, NZ), jnp.float32)],
+            scratch_shapes=[
+                pltpu.VMEM((4, NL, NZ), jnp.float32),
+                pltpu.VMEM((2, owners * cols, 2 * NZ), jnp.bfloat16),
+            ],
         ),
         out_shape=[
             jax.ShapeDtypeStruct((each, 2, half, NZ), jnp.float32),
@@ -491,7 +514,7 @@
         cost_estimate=pl.CostEstimate(
             flops=8 * each * NL * NL * NZ, bytes_accessed=each * 1200000, transcendentals=0
         ),
-    )(coil_id, early, late, maps, *tables)
+    )(where, early, near, *across, maps, *tables)
 
 
 def sum_kernel(total_ref, own_ref, other_ref, out_ref):
@@ -504,10 +527,10 @@
             )
 
 
-def sum_stage(total, own, other, piece):
+def sum_stage(total, own, other, base_row):
     each, _, half = own.shape[:3]
-    rows = 4
-    base = piece * each // rows
+    rows = 2
+    base = base_row // rows
     return pl.pallas_call(
         sum_kernel,
         grid=(each // rows,),
@@ -549,7 +572,7 @@
     local_cols = NL // pen_count
     pen_id = lax.axis_index("pen")
     coil_id = lax.axis_index("coil")
-    chunks, row_chunks = 2, 4
+    chunks = 2
     chunk_cols = local_cols // chunks
     image = image_field.reshape(own_rows, 2 * NL, NZ)
     maps = coil_maps.reshape(own_rows, 2 * NL, NZ)
@@ -562,7 +585,6 @@
     tables_rows = pair_tables(1.0 / 16, split, natural)
     tables_cols = pair_tables(1.0 / 32, natural, natural)
     tables_back = pair_tables(1.0 / 16, natural, split)
-    tables_back = [jnp.roll(table, -coil_id * (NL // 2), 0) for table in tables_back]
     per_col = NL // TILE
     plan = block_plan(tile_of_block, pen_id, block_count // 2, 2 * per_col)
 
@@ -576,26 +598,77 @@
         spectra = row_spectra(image, maps, tables_rows, chunk, chunks)
         spectra = spectra.reshape(pen_count, 2 * chunk_cols, own_rows, NZ)
         arrived.append(exchange(spectra))
-    back = []
-    for chunk in range(chunks):
-        pieces = 1 if chunk == 0 else row_chunks
-        result = column_stage(
-            arrived[chunk], tables_cols, kernels, sample_rows, plan, chunk, chunks, pieces
+    where = jnp.stack([coil_id, pen_id]).astype(jnp.int32)
+    plan = plan + (where[1:],)
+    unit = own_rows // 32
+    sizes = [10 * unit, 10 * unit, 6 * unit, 6 * unit]
+    row_pieces = tuple((sum(sizes[:n]), sizes[n]) for n in range(len(sizes)))
+    near_count = pen_count // 2
+    crosses = tuple(range(near_count, pen_count))
+    near_groups = [list(range(near_count)), list(range(near_count, pen_count))]
+    cut = sizes[0] + sizes[1]
+    halves = ((0, cut), (cut, own_rows - cut))
+
+    first = column_stage(
+        arrived[0],
+        tables_cols,
+        kernels,
+        sample_rows,
+        plan,
+        0,
+        chunks,
+        tuple(("all", 0, pen_count, base_row, each) for base_row, each in halves),
+    )
+    early = []
+    for part, (base_row, each) in enumerate(halves):
+        early.append(exchange(first[part].reshape(pen_count, each, 2, chunk_cols, NZ)))
+    jobs = [("near", near_count, near_count, 0, own_rows)]
+    for base_row, each in row_pieces:
+        jobs += [("cross", which, 1, base_row, each) for which in crosses]
+    result = column_stage(
+        arrived[1], tables_cols, kernels, sample_rows, plan, 1, chunks, tuple(jobs)
+    )
+    near = lax.all_to_all(
+        result[0].reshape(near_count, own_rows, 2, chunk_cols, NZ),
+        "pen",
+        split_axis=0,
+        concat_axis=0,
+        axis_index_groups=near_groups,
+        tiled=True,
+    )
+    across = []
+    for piece, (base_row, each) in enumerate(row_pieces):
+        across.append(
+            [
+                lax.ppermute(
+                    result[1 + piece * near_count + place].reshape(each, 2, chunk_cols, NZ),
+                    "pen",
+                    [(i, i ^ which) for i in range(pen_count)],
+                )
+                for place, which in enumerate(crosses)
+            ]
         )
-        got = []
-        for piece in range(pieces):
-            one = result[piece].reshape(pen_count, own_rows // pieces, 2, chunk_cols, NZ)
-            got.append(exchange(one))
-        back.append(got)
-    total = variation_stage(image, above, below, jnp.stack([coil_id, pen_id]).astype(jnp.int32))
+    shift = coil_id * (NL // 2)
+    back_cos = jnp.roll(tables_back[0], -shift, 0)
+    later_shift = lax.optimization_barrier((shift, result[-1]))[0]
+    back_sin = jnp.roll(tables_back[1], -later_shift, 0)
+    total = variation_stage(image, above, below, where)
     side_maps = maps.reshape(own_rows, 2, NL, NZ)
-    coil_vec = coil_id.reshape(1).astype(jnp.int32)
-    for piece in range(row_chunks):
+    for piece, (base_row, each) in enumerate(row_pieces):
+        part = 0 if base_row < cut else 1
         own, send = image_stage(
-            coil_vec, back[0][0], back[1][piece], side_maps, tables_back, piece
+            where,
+            early[part],
+            near,
+            crosses,
+            across[piece],
+            side_maps,
+            (back_cos, back_sin),
+            base_row,
+            base_row - halves[part][0],
         )
         other = lax.ppermute(send, "coil", [(0, 1), (1, 0)])
-        total = sum_stage(total, own, other, piece)
+        total = sum_stage(total, own, other, base_row)
     return total.reshape(own_rows, NL // 2, 2, NZ)
 
 

time: 547 us -> 570 us (1.042)
  blocking collectives: 172 us -> 64.6 us
  starting transfers between devices: 46 us -> 117 us
  waiting for transfers between devices: 107 us -> 151 us
  Pallas kernels: 210 us -> 225 us
    all_to_all x3 -> x1, blocking collectives: 172 us -> 64.6 us  [exchange(): return lax.all_to_all(array, 'pen', split_axis=0, concat_axis=0, tiled=True)]
    ppermute x0 -> x32, starting transfers between devices: none -> 58.2 us  [gradient_parts(): lax.ppermute(result[1 + piece * near_count + place].reshape(each, 2, chun...]
    ppermute x0 -> x32, waiting for transfers between devices: none -> 55.3 us  [gradient_parts(): lax.ppermute(result[1 + piece * near_count + place].reshape(each, 2, chun...]
    all_to_all x0 -> x1, starting transfers between devices: none -> 18.7 us  [gradient_parts(): lax.all_to_all(result[0].reshape(near_count, own_rows, 2, chunk_cols, NZ)...]
    pallas_call x6, Pallas kernels: 127 us -> 137 us  [the longest x2 108 us: column_stage(): pl.pallas_call(functools.partial(columns_kernel, chunk * steps, jobs), gr...]
    ppermute x4, waiting for transfers between devices: 20.3 us -> 10.4 us  [gradient_parts(): other = lax.ppermute(send, 'coil', [(0, 1), (1, 0)])]
    all_to_all x4 -> x3, starting transfers between devices: 37.5 us -> 32.5 us  [exchange(): return lax.all_to_all(array, 'pen', split_axis=0, concat_axis=0, tiled=True)]
    all_to_all x4 -> x3, waiting for transfers between devices: 84.3 us -> 82 us  [exchange(): return lax.all_to_all(array, 'pen', split_axis=0, concat_axis=0, tiled=True)]
  transfers between devices with their start and end apart: 10 -> 42, of which waited for: 5 -> 13; matrix products, arithmetic and copies ran while one was open for 1% -> 1% of each run, Pallas kernels for 35% -> 36%
where the time goes in v2:
time: 570 us; the launch traced here: 569 us
  Pallas kernels  225 us (39%)
  waiting for transfers between devices  151 us (26%)
  starting transfers between devices  117 us (21%)
  blocking collectives  64.6 us (11%)
  local copies, waits for them, and re-layouts  8.17 us (1%)
    pallas_call x2, Pallas kernels, column_stage(): pl.pallas_call(functools.partial(columns_kernel, chunk * steps, jobs), gr...  108 us
    all_to_all x3, waiting for transfers between devices, exchange(): return lax.all_to_all(array, 'pen', split_axis=0, concat_axis=0, tiled=True)  82 us
    all_to_all x1, blocking collectives, exchange(): return lax.all_to_all(array, 'pen', split_axis=0, concat_axis=0, tiled=True)  64.6 us
    ppermute x32, starting transfers between devices, gradient_parts(): lax.ppermute(result[1 + piece * near_count + place].reshape(each, 2, chun...  58.2 us
    ppermute x32, waiting for transfers between devices, gradient_parts(): lax.ppermute(result[1 + piece * near_count + place].reshape(each, 2, chun...  55.3 us
    pallas_call x2, Pallas kernels, row_spectra(): pl.pallas_call(rows_kernel, grid=(rows // 16, 2), in_specs=[pl.BlockSpec(...  35.8 us
    pallas_call x1, Pallas kernels, variation_stage(): pl.pallas_call(variation_kernel, grid_spec=pltpu.PrefetchScalarGridSpec(n...  33.1 us
    all_to_all x3, starting transfers between devices, exchange(): return lax.all_to_all(array, 'pen', split_axis=0, concat_axis=0, tiled=True)  32.5 us
  transfers between devices with their start and end apart: 42, of which 13 were waited for; matrix products, arithmetic and copies ran while one was open for 1% of the time, Pallas kernels for 36%

profile of v2, /device:TPU:0, one launch (start us, length us, event | category | flops | bytes accessed | tf_op | source)
XLA Modules:
  0.0 568.9 jit_solution(9930214276326591244)
XLA Ops:
  0.0 17.9 %shard_map.111 = bf16[512,32,128]{2,1,0:T(8,128)(2,1)} custom-call(f32[32,1024,128]{2,1,0:T(8,128)} %bitcast.52, bf16[32,1024,128]{2,1,0:T(8,128)(2,1)} %bitcast.46, bf16[512,512]{1,0:T(8,128)(2,1)} %constant.61.clone.cos_ref, bf16[512,512]{1,0:T(8,128)(2,1)} %constant.62.clone.sin_ref), custom_call_target="tpu_custom_call" | custom-call | flops 4294967296 | bytes 30000000 | tf_op jit(solution)/shard_map/pallas_call | solution.py:210
  17.9 7.4 %all-to-all-start.2 = ((bf16[16,32,32,128]{3,2,1,0:T(8,128)(2,1)}), bf16[16,32,32,128]{3,2,1,0:T(8,128)(2,1)}, u32[]{:S(2)}, u32[]{:S(2)}) async-start(bf16[16,32,32,128]{3,2,1,0:T(8,128)(2,1)} %bitcast.57), calls=%async_computation.2 | async-start | bytes 8388608 | tf_op jit(solution)/shard_map/all_to_all | solution.py:592
  25.3 17.9 %shard_map.109 = bf16[512,32,128]{2,1,0:T(8,128)(2,1)} custom-call(f32[32,1024,128]{2,1,0:T(8,128)} %bitcast.53, bf16[32,1024,128]{2,1,0:T(8,128)(2,1)} %bitcast.47, bf16[512,512]{1,0:T(8,128)(2,1)} %constant.61.clone.cos_ref, bf16[512,512]{1,0:T(8,128)(2,1)} %constant.62.clone.sin_ref), custom_call_target="tpu_custom_call" | custom-call | flops 4294967296 | bytes 30000000 | tf_op jit(solution)/shard_map/pallas_call | solution.py:210
  43.2 59.6 %all-to-all-done.2.spec_ref = bf16[16,32,32,128]{3,2,1,0:T(8,128)(2,1)} async-done(((bf16[16,32,32,128]{3,2,1,0:T(8,128)(2,1)}), bf16[16,32,32,128]{3,2,1,0:T(8,128)(2,1)}, u32[]{:S(2)}, u32[]{:S(2)}) %all-to-all-start.2) | async-done | bytes 4194336 | tf_op jit(solution)/shard_map/all_to_all | solution.py:592
  102.9 19.8 %all-to-all-start = ((bf16[16,32,32,128]{3,2,1,0:T(8,128)(2,1)}), bf16[16,32,32,128]{3,2,1,0:T(8,128)(2,1)}, u32[]{:S(2)}, u32[]{:S(2)}) async-start(bf16[16,32,32,128]{3,2,1,0:T(8,128)(2,1)} %bitcast.56), calls=%async_computation | async-start | bytes 8388608 | tf_op jit(solution)/shard_map/all_to_all | solution.py:592
  124.9 53.0 %shard_map.112 = (bf16[512,16,128]{2,1,0:T(8,128)(2,1)}, bf16[20,16,128]{2,1,0:T(8,128)(2,1)}, bf16[20,16,128]{2,1,0:T(8,128)(2,1)}, bf16[20,16,128]{2,1,0:T(8,1...) custom-call(s32[256]{0:T(256)} %get-tuple-element.95.order_ref, ...), custom_call_target="tpu_custom_call" | custom-call | flops 30000001024 | bytes 20000000 | tf_op jit(solution)/shard_map/pallas_call | solution.py:389
  177.9 22.3 %all-to-all-done.spec_ref = bf16[16,32,32,128]{3,2,1,0:T(8,128)(2,1)} async-done(((bf16[16,32,32,128]{3,2,1,0:T(8,128)(2,1)}), bf16[16,32,32,128]{3,2,1,0:T(8,128)(2,1)}, u32[]{:S(2)}, u32[]{:S(2)}) %all-to-all-start) | async-done | bytes 4194336 | tf_op jit(solution)/shard_map/all_to_all | solution.py:592
  200.3 18.7 %all-to-all-start.3 = ((bf16[8,32,2,16,128]{4,3,2,1,0:T(8,128)(2,1)}), bf16[8,32,2,16,128]{4,3,2,1,0:T(8,128)(2,1)S(1)}, u32[]{:S(2)}, u32[]{:S(2)}) async-start(bf16[8,32,2,16,128]{4,3,2,1,0:T(8,128)(2,1)} %bitcast.59), calls=%async_computation.3 | async-start | bytes 4194304 | tf_op jit(solution)/shard_map/all_to_all | solution.py:631
  218.9 54.5 %shard_map.110 = (bf16[640,16,128]{2,1,0:T(8,128)(2,1)}, bf16[384,16,128]{2,1,0:T(8,128)(2,1)}) custom-call(s32[256]{0:T(256)} %get-tuple-element.95.order_ref, s32[256]{0:T(256)} %and_select_fusion.local_ref, s32[17]{0:T(128)} %convert_reduce_fusion.1.bounds_ref, s32[1]{0:T(128)} %bitcast.1.pen_ref, bf16[16,32,32,128]{3,2,1,0:T(8,128)(2,1)} %all-to-all-done.spec_ref, ...), custom_call_target="tpu_custom_call" | custom-call | flops 30000001024 | bytes 20000000 | tf_op jit(solution)/shard_map/pallas_call | solution.py:389
  273.5 64.6 %all_to_all.25.early_ref = bf16[16,20,2,16,128]{4,3,2,1,0:T(8,128)(2,1)} all-to-all(bf16[16,20,2,16,128]{4,3,2,1,0:T(8,128)(2,1)} %bitcast.58), channel_id=1, replica_groups=mesh['pen'=16,'coil'=2] {'pen'}, dimensions={0} | all-to-all | bytes 5242880 | tf_op jit(solution)/shard_map/all_to_all | solution.py:592
  338.1 5.2 all-to-all-start.4
  343.4 2.8 collective-permute-start.20
  352.1 36.6 %collective-permute-done.20.rest_0_ = bf16[6,2,16,128]{3,2,1,0:T(8,128)(2,1)S(1)} collective-permute-done((bf16[6,2,16,128]{3,2,1,0:T(8,128)(2,1)S(1)}, bf16[6,2,16,128]{3,2,1,0:T(8,128)(2,1)S(1)}, u32[]{:S(2)}, u32[]{:S(2)}) %collective-permute-start.20) | collective-permute-done | bytes 49184 | tf_op jit(solution)/shard_map/ppermute | solution.py:643
  390.6 3.4 collective-permute-done.22.rest_2_
  399.0 3.9 collective-permute-start.13
  404.6 8.2 %collective-permute-done.4.rest_2_ = bf16[10,2,16,128]{3,2,1,0:T(8,128)(2,1)S(1)} collective-permute-done((bf16[10,2,16,128]{3,2,1,0:T(8,128)(2,1)}, bf16[10,2,16,128]{3,2,1,0:T(8,128)(2,1)S(1)}, u32[]{:S(2)}, u32[]{:S(2)}) %collective-permute-start.4) | collective-permute-done | bytes 81952 | tf_op jit(solution)/shard_map/ppermute | solution.py:643
  425.5 6.2 %collective-permute-start.7 = (bf16[10,2,16,128]{3,2,1,0:T(8,128)(2,1)}, bf16[10,2,16,128]{3,2,1,0:T(8,128)(2,1)S(1)}, u32[]{:S(2)}, u32[]{:S(2)}) collective-permute-start(bf16[10,2,16,128]{3,2,1,0:T(8,128)(2,1)} %bitcast.65), channel_id=1, source_target_pairs={{0,26},{2,24},{4,30},{6,28},{8,18},{10,16},{12,22},{14,20},{16,10}... | collective-permute-start | bytes 245768 | tf_op jit(solution)/shard_map/ppermute | solution.py:643
  432.9 8.5 %shard_map.115 = (f32[10,2,256,128]{3,2,1,0:T(8,128)}, bf16[10,2,256,128]{3,2,1,0:T(8,128)(2,1)}) custom-call(s32[2]{0:T(128)} %pad_add_fusion.where_ref, bf16[16,20,2,16,128]{4,3,2,1,0:T(8,128)(2,1)} %all_to_all.25.early_ref, bf16[8,32,2,16,128]{4,3,2,1,0:T(8,128)(2,1)} %copy-done, bf16[10,2,16,128]{3,2,1,0:T(8,128)(2,1)} %copy-done.8, ...), custom_call_target="tpu_custom_call" | custom-call | flops 2684354560 | bytes 12000000 | tf_op jit(solution)/shard_map/pallas_call | solution.py:482
  445.9 3.7 collective-permute-start.27
  449.5 6.0 %collective-permute-start.29 = (bf16[6,2,16,128]{3,2,1,0:T(8,128)(2,1)S(1)}, bf16[6,2,16,128]{3,2,1,0:T(8,128)(2,1)S(1)}, u32[]{:S(2)}, u32[]{:S(2)}) collective-permute-start(bf16[6,2,16,128]{3,2,1,0:T(8,128)(2,1)S(1)} %bitcast.84), channel_id=1, source_target_pairs={{0,16},{2,18},{4,20},{6,22},{8,24},{10,26},{12,28},{14,30},{16,0},... | collective-permute-start | bytes 147464 | tf_op jit(solution)/shard_map/ppermute | solution.py:643
  455.8 3.6 collective-permute-start.31
  459.5 8.4 %shard_map.113 = (f32[10,2,256,128]{3,2,1,0:T(8,128)}, bf16[10,2,256,128]{3,2,1,0:T(8,128)(2,1)}) custom-call(s32[2]{0:T(128)} %pad_add_fusion.where_ref, bf16[16,20,2,16,128]{4,3,2,1,0:T(8,128)(2,1)} %all_to_all.25.early_ref, bf16[8,32,2,16,128]{4,3,2,1,0:T(8,128)(2,1)} %copy-done, bf16[10,2,16,128]{3,2,1,0:T(8,128)(2,1)} %copy-done.5, ...), custom_call_target="tpu_custom_call" | custom-call | flops 2684354560 | bytes 12000000 | tf_op jit(solution)/shard_map/pallas_call | solution.py:482
  480.7 3.0 collective-permute-start.36
  483.7 6.2 %shard_map.117 = (f32[6,2,256,128]{3,2,1,0:T(8,128)}, bf16[6,2,256,128]{3,2,1,0:T(8,128)(2,1)}) custom-call(s32[2]{0:T(128)} %pad_add_fusion.where_ref, bf16[16,12,2,16,128]{4,3,2,1,0:T(8,128)(2,1)} %all-to-all-done.4.early_ref, bf16[8,32,2,16,128]{4,3,2,1,0:T(8,128)(2,1)} %copy-done, bf16[6,2,16,128]{3,2,1,0:T(8,128)(2,1)} %copy-done.21, ...), custom_call_target="tpu_custom_call" | custom-call | flops 1610612736 | bytes 7200000 | tf_op jit(solution)/shard_map/pallas_call | solution.py:482
  492.0 6.2 %shard_map.119 = (f32[6,2,256,128]{3,2,1,0:T(8,128)}, bf16[6,2,256,128]{3,2,1,0:T(8,128)(2,1)}) custom-call(s32[2]{0:T(128)} %pad_add_fusion.where_ref, bf16[16,12,2,16,128]{4,3,2,1,0:T(8,128)(2,1)} %all-to-all-done.4.early_ref, bf16[8,32,2,16,128]{4,3,2,1,0:T(8,128)(2,1)} %copy-done, bf16[6,2,16,128]{3,2,1,0:T(8,128)(2,1)} %copy-done.27, ...), custom_call_target="tpu_custom_call" | custom-call | flops 1610612736 | bytes 7200000 | tf_op jit(solution)/shard_map/pallas_call | solution.py:482
  500.1 2.8 collective-permute-done.1.below_ref
  502.9 33.1 %variation.1.total_ref = f32[32,512,128]{2,1,0:T(8,128)} custom-call(s32[2]{0:T(128)} %pad_add_fusion.where_ref, f32[32,1024,128]{2,1,0:T(8,128)} %bitcast.54, f32[32,1024,128]{2,1,0:T(8,128)} %bitcast.55, f32[1,1024,128]{2,1,0:T(8,128)} %collective-permute-done.above_ref, f32[1,1024,128]{2,1,0:T(8,128)} %collective-permute-done.1.below_ref), custom_call_target="tpu_custom_call" | custom-call | flops 83886080 | bytes 60000000 | tf_op jit(solution)/shard_map/variation/pallas_call | solution.py:770
  537.1 5.7 %shard_map.114.total_ref = f32[32,512,128]{2,1,0:T(8,128)} custom-call(f32[32,512,128]{2,1,0:T(8,128)} %variation.1.total_ref, f32[10,2,256,128]{3,2,1,0:T(8,128)} %get-tuple-element.62.own_ref, bf16[10,2,256,128]{3,2,1,0:T(8,128)(2,1)} %copy-done.2), custom_call_target="tpu_custom_call", output_to_operand_aliasing={{}: (0, {})} | custom-call | flops 1310720 | bytes 10000000 | tf_op jit(solution)/shard_map/pallas_call | solution.py:534
  543.9 5.7 %shard_map.116.total_ref = f32[32,512,128]{2,1,0:T(8,128)} custom-call(f32[32,512,128]{2,1,0:T(8,128)} %shard_map.114.total_ref, f32[10,2,256,128]{3,2,1,0:T(8,128)} %get-tuple-element.72.own_ref, bf16[10,2,256,128]{3,2,1,0:T(8,128)(2,1)} %copy-done.1), custom_call_target="tpu_custom_call", output_to_operand_aliasing={{}: (0, {})} | custom-call | flops 1310720 | bytes 10000000 | tf_op jit(solution)/shard_map/pallas_call | solution.py:534
  550.6 3.9 shard_map.118.total_ref
  554.5 10.4 %collective-permute-done.37.other_ref = bf16[6,2,256,128]{3,2,1,0:T(8,128)(2,1)} collective-permute-done((bf16[6,2,256,128]{3,2,1,0:T(8,128)(2,1)}, bf16[6,2,256,128]{3,2,1,0:T(8,128)(2,1)}, u32[]{:S(2)}, u32[]{:S(2)}) %collective-permute-start.37) | collective-permute-done | bytes 786464 | tf_op jit(solution)/shard_map/ppermute | solution.py:670
  564.9 3.9 shard_map.120
  (173 shorter events, 54.8 us)
Async XLA Ops:
  17.9 85.0 %all-to-all-start.2 = ((bf16[16,32,32,128]{3,2,1,0:T(8,128)(2,1)}), bf16[16,32,32,128]{3,2,1,0:T(8,128)(2,1)}, u32[]{:S(2)}, u32[]{:S(2)}) async-start(bf16[16,32,32,128]{3,2,1,0:T(8,128)(2,1)} %bitcast.57), calls=%async_computation.2 | async-start | bytes 8388608 | tf_op jit(solution)/shard_map/all_to_all | solution.py:592
  102.9 97.4 %all-to-all-start = ((bf16[16,32,32,128]{3,2,1,0:T(8,128)(2,1)}), bf16[16,32,32,128]{3,2,1,0:T(8,128)(2,1)}, u32[]{:S(2)}, u32[]{:S(2)}) async-start(bf16[16,32,32,128]{3,2,1,0:T(8,128)(2,1)} %bitcast.56), calls=%async_computation | async-start | bytes 8388608 | tf_op jit(solution)/shard_map/all_to_all | solution.py:592
  200.3 73.2 %all-to-all-start.3 = ((bf16[8,32,2,16,128]{4,3,2,1,0:T(8,128)(2,1)}), bf16[8,32,2,16,128]{4,3,2,1,0:T(8,128)(2,1)S(1)}, u32[]{:S(2)}, u32[]{:S(2)}) async-start(bf16[8,32,2,16,128]{4,3,2,1,0:T(8,128)(2,1)} %bitcast.59), calls=%async_computation.3 | async-start | bytes 4194304 | tf_op jit(solution)/shard_map/all_to_all | solution.py:631
  338.1 145.5 %all-to-all-start.4 = ((bf16[16,12,2,16,128]{4,3,2,1,0:T(8,128)(2,1)}), bf16[16,12,2,16,128]{4,3,2,1,0:T(8,128)(2,1)}, u32[]{:S(2)}, u32[]{:S(2)}) async-start(bf16[16,12,2,16,128]{4,3,2,1,0:T(8,128)(2,1)} %bitcast.60), calls=%async_computation.4 | async-start | bytes 3145728 | tf_op jit(solution)/shard_map/all_to_all | solution.py:592
  343.4 45.3 %collective-permute-start.20 = (bf16[6,2,16,128]{3,2,1,0:T(8,128)(2,1)S(1)}, bf16[6,2,16,128]{3,2,1,0:T(8,128)(2,1)S(1)}, u32[]{:S(2)}, u32[]{:S(2)}) collective-permute-start(bf16[6,2,16,128]{3,2,1,0:T(8,128)(2,1)S(1)} %bitcast.89), channel_id=1, source_target_pairs={{0,16},{2,18},{4,20},{6,22},{8,24},{10,26},{12,28},{14,30},{16,0},... | collective-permute-start | bytes 147464 | tf_op jit(solution)/shard_map/ppermute | solution.py:643
  346.2 43.9 %collective-permute-start.21 = (bf16[6,2,16,128]{3,2,1,0:T(8,128)(2,1)S(1)}, bf16[6,2,16,128]{3,2,1,0:T(8,128)(2,1)S(1)}, u32[]{:S(2)}, u32[]{:S(2)}) collective-permute-start(bf16[6,2,16,128]{3,2,1,0:T(8,128)(2,1)S(1)} %bitcast.88), channel_id=1, source_target_pairs={{0,18},{2,16},{4,22},{6,20},{8,26},{10,24},{12,30},{14,28},{16,2},... | collective-permute-start | bytes 147464 | tf_op jit(solution)/shard_map/ppermute | solution.py:643
  346.2 52.8 %collective-permute-start.2 = (bf16[10,2,16,128]{3,2,1,0:T(8,128)(2,1)}, bf16[10,2,16,128]{3,2,1,0:T(8,128)(2,1)S(1)}, u32[]{:S(2)}, u32[]{:S(2)}) collective-permute-start(bf16[10,2,16,128]{3,2,1,0:T(8,128)(2,1)} %bitcast.11), channel_id=1, source_target_pairs={{0,16},{2,18},{4,20},{6,22},{8,24},{10,26},{12,28},{14,30},{16,0},... | collective-permute-start | bytes 245768 | tf_op jit(solution)/shard_map/ppermute | solution.py:643
  348.6 45.5 %collective-permute-start.22 = (bf16[6,2,16,128]{3,2,1,0:T(8,128)(2,1)}, bf16[6,2,16,128]{3,2,1,0:T(8,128)(2,1)S(1)}, u32[]{:S(2)}, u32[]{:S(2)}) collective-permute-start(bf16[6,2,16,128]{3,2,1,0:T(8,128)(2,1)} %bitcast.31), channel_id=1, source_target_pairs={{0,20},{2,22},{4,16},{6,18},{8,28},{10,30},{12,24},{14,26},{16,4},... | collective-permute-start | bytes 147464 | tf_op jit(solution)/shard_map/ppermute | solution.py:643
  350.0 44.0 %collective-permute-start.23 = (bf16[6,2,16,128]{3,2,1,0:T(8,128)(2,1)}, bf16[6,2,16,128]{3,2,1,0:T(8,128)(2,1)S(1)}, u32[]{:S(2)}, u32[]{:S(2)}) collective-permute-start(bf16[6,2,16,128]{3,2,1,0:T(8,128)(2,1)} %bitcast.32), channel_id=1, source_target_pairs={{0,22},{2,20},{4,18},{6,16},{8,30},{10,28},{12,26},{14,24},{16,6},... | collective-permute-start | bytes 147464 | tf_op jit(solution)/shard_map/ppermute | solution.py:643
  394.1 18.8 %collective-permute-start.4 = (bf16[10,2,16,128]{3,2,1,0:T(8,128)(2,1)}, bf16[10,2,16,128]{3,2,1,0:T(8,128)(2,1)S(1)}, u32[]{:S(2)}, u32[]{:S(2)}) collective-permute-start(bf16[10,2,16,128]{3,2,1,0:T(8,128)(2,1)} %bitcast.76), channel_id=1, source_target_pairs={{0,20},{2,22},{4,16},{6,18},{8,28},{10,30},{12,24},{14,26},{16,4},... | collective-permute-start | bytes 245768 | tf_op jit(solution)/shard_map/ppermute | solution.py:643
  396.1 18.4 %collective-permute-start.11 = (bf16[10,2,16,128]{3,2,1,0:T(8,128)(2,1)}, bf16[10,2,16,128]{3,2,1,0:T(8,128)(2,1)S(1)}, u32[]{:S(2)}, u32[]{:S(2)}) collective-permute-start(bf16[10,2,16,128]{3,2,1,0:T(8,128)(2,1)} %bitcast.75), channel_id=1, source_target_pairs={{0,16},{2,18},{4,20},{6,22},{8,24},{10,26},{12,28},{14,30},{16,0},... | collective-permute-start | bytes 245768 | tf_op jit(solution)/shard_map/ppermute | solution.py:643
  398.2 16.9 %collective-permute-start.12 = (bf16[10,2,16,128]{3,2,1,0:T(8,128)(2,1)}, bf16[10,2,16,128]{3,2,1,0:T(8,128)(2,1)S(1)}, u32[]{:S(2)}, u32[]{:S(2)}) collective-permute-start(bf16[10,2,16,128]{3,2,1,0:T(8,128)(2,1)} %bitcast.74), channel_id=1, source_target_pairs={{0,18},{2,16},{4,22},{6,20},{8,26},{10,24},{12,30},{14,28},{16,2},... | collective-permute-start | bytes 245768 | tf_op jit(solution)/shard_map/ppermute | solution.py:643
  399.0 19.9 %collective-permute-start.13 = (bf16[10,2,16,128]{3,2,1,0:T(8,128)(2,1)}, bf16[10,2,16,128]{3,2,1,0:T(8,128)(2,1)S(1)}, u32[]{:S(2)}, u32[]{:S(2)}) collective-permute-start(bf16[10,2,16,128]{3,2,1,0:T(8,128)(2,1)} %bitcast.73), channel_id=1, source_target_pairs={{0,20},{2,22},{4,16},{6,18},{8,28},{10,30},{12,24},{14,26},{16,4},... | collective-permute-start | bytes 245768 | tf_op jit(solution)/shard_map/ppermute | solution.py:643
  404.6 19.4 %collective-permute-start.14 = (bf16[10,2,16,128]{3,2,1,0:T(8,128)(2,1)}, bf16[10,2,16,128]{3,2,1,0:T(8,128)(2,1)S(1)}, u32[]{:S(2)}, u32[]{:S(2)}) collective-permute-start(bf16[10,2,16,128]{3,2,1,0:T(8,128)(2,1)} %bitcast.72), channel_id=1, source_target_pairs={{0,22},{2,20},{4,18},{6,16},{8,30},{10,28},{12,26},{14,24},{16,6},... | collective-permute-start | bytes 245768 | tf_op jit(solution)/shard_map/ppermute | solution.py:643
  415.1 16.6 %collective-permute-start.17 = (bf16[10,2,16,128]{3,2,1,0:T(8,128)(2,1)}, bf16[10,2,16,128]{3,2,1,0:T(8,128)(2,1)S(1)}, u32[]{:S(2)}, u32[]{:S(2)}) collective-permute-start(bf16[10,2,16,128]{3,2,1,0:T(8,128)(2,1)} %bitcast.69), channel_id=1, source_target_pairs={{0,28},{2,30},{4,24},{6,26},{8,20},{10,22},{12,16},{14,18},{16,12}... | collective-permute-start | bytes 245768 | tf_op jit(solution)/shard_map/ppermute | solution.py:643
  419.0 12.8 %collective-permute-start.18 = (bf16[10,2,16,128]{3,2,1,0:T(8,128)(2,1)}, bf16[10,2,16,128]{3,2,1,0:T(8,128)(2,1)S(1)}, u32[]{:S(2)}, u32[]{:S(2)}) collective-permute-start(bf16[10,2,16,128]{3,2,1,0:T(8,128)(2,1)} %bitcast.68), channel_id=1, source_target_pairs={{0,30},{2,28},{4,26},{6,24},{8,22},{10,20},{12,18},{14,16},{16,14}... | collective-permute-start | bytes 245768 | tf_op jit(solution)/shard_map/ppermute | solution.py:643
  424.0 19.3 %collective-permute-start.5 = (bf16[10,2,16,128]{3,2,1,0:T(8,128)(2,1)}, bf16[10,2,16,128]{3,2,1,0:T(8,128)(2,1)S(1)}, u32[]{:S(2)}, u32[]{:S(2)}) collective-permute-start(bf16[10,2,16,128]{3,2,1,0:T(8,128)(2,1)} %bitcast.67), channel_id=1, source_target_pairs={{0,22},{2,20},{4,18},{6,16},{8,30},{10,28},{12,26},{14,24},{16,6},... | collective-permute-start | bytes 245768 | tf_op jit(solution)/shard_map/ppermute | solution.py:643
  424.0 21.9 %collective-permute-start.6 = (bf16[10,2,16,128]{3,2,1,0:T(8,128)(2,1)}, bf16[10,2,16,128]{3,2,1,0:T(8,128)(2,1)S(1)}, u32[]{:S(2)}, u32[]{:S(2)}) collective-permute-start(bf16[10,2,16,128]{3,2,1,0:T(8,128)(2,1)} %bitcast.66), channel_id=1, source_target_pairs={{0,24},{2,26},{4,28},{6,30},{8,16},{10,18},{12,20},{14,22},{16,8},... | collective-permute-start | bytes 245768 | tf_op jit(solution)/shard_map/ppermute | solution.py:643
  425.5 24.0 %collective-permute-start.7 = (bf16[10,2,16,128]{3,2,1,0:T(8,128)(2,1)}, bf16[10,2,16,128]{3,2,1,0:T(8,128)(2,1)S(1)}, u32[]{:S(2)}, u32[]{:S(2)}) collective-permute-start(bf16[10,2,16,128]{3,2,1,0:T(8,128)(2,1)} %bitcast.65), channel_id=1, source_target_pairs={{0,26},{2,24},{4,30},{6,28},{8,18},{10,16},{12,22},{14,20},{16,10}... | collective-permute-start | bytes 245768 | tf_op jit(solution)/shard_map/ppermute | solution.py:643
  431.7 23.8 %collective-permute-start.8 = (bf16[10,2,16,128]{3,2,1,0:T(8,128)(2,1)S(1)}, bf16[10,2,16,128]{3,2,1,0:T(8,128)(2,1)S(1)}, u32[]{:S(2)}, u32[]{:S(2)}) collective-permute-start(bf16[10,2,16,128]{3,2,1,0:T(8,128)(2,1)S(1)} %bitcast.64), channel_id=1, source_target_pairs={{0,28},{2,30},{4,24},{6,26},{8,20},{10,22},{12,16},{14,18},{16,12}... | collective-permute-start | bytes 245768 | tf_op jit(solution)/shard_map/ppermute | solution.py:643
  431.8 24.0 %collective-permute-start.9 = (bf16[10,2,16,128]{3,2,1,0:T(8,128)(2,1)}, bf16[10,2,16,128]{3,2,1,0:T(8,128)(2,1)S(1)}, u32[]{:S(2)}, u32[]{:S(2)}) collective-permute-start(bf16[10,2,16,128]{3,2,1,0:T(8,128)(2,1)} %bitcast.18), channel_id=1, source_target_pairs={{0,30},{2,28},{4,26},{6,24},{8,22},{10,20},{12,18},{14,16},{16,14}... | collective-permute-start | bytes 245768 | tf_op jit(solution)/shard_map/ppermute | solution.py:643
  443.3 24.6 %collective-permute-start.26 = (bf16[6,2,16,128]{3,2,1,0:T(8,128)(2,1)S(1)}, bf16[6,2,16,128]{3,2,1,0:T(8,128)(2,1)S(1)}, u32[]{:S(2)}, u32[]{:S(2)}) collective-permute-start(bf16[6,2,16,128]{3,2,1,0:T(8,128)(2,1)S(1)} %bitcast.86), channel_id=1, source_target_pairs={{0,28},{2,30},{4,24},{6,26},{8,20},{10,22},{12,16},{14,18},{16,12}... | collective-permute-start | bytes 147464 | tf_op jit(solution)/shard_map/ppermute | solution.py:643
  445.9 22.2 %collective-permute-start.27 = (bf16[6,2,16,128]{3,2,1,0:T(8,128)(2,1)S(1)}, bf16[6,2,16,128]{3,2,1,0:T(8,128)(2,1)S(1)}, u32[]{:S(2)}, u32[]{:S(2)}) collective-permute-start(bf16[6,2,16,128]{3,2,1,0:T(8,128)(2,1)S(1)} %bitcast.85), channel_id=1, source_target_pairs={{0,30},{2,28},{4,26},{6,24},{8,22},{10,20},{12,18},{14,16},{16,14}... | collective-permute-start | bytes 147464 | tf_op jit(solution)/shard_map/ppermute | solution.py:643
  449.5 20.7 %collective-permute-start.29 = (bf16[6,2,16,128]{3,2,1,0:T(8,128)(2,1)S(1)}, bf16[6,2,16,128]{3,2,1,0:T(8,128)(2,1)S(1)}, u32[]{:S(2)}, u32[]{:S(2)}) collective-permute-start(bf16[6,2,16,128]{3,2,1,0:T(8,128)(2,1)S(1)} %bitcast.84), channel_id=1, source_target_pairs={{0,16},{2,18},{4,20},{6,22},{8,24},{10,26},{12,28},{14,30},{16,0},... | collective-permute-start | bytes 147464 | tf_op jit(solution)/shard_map/ppermute | solution.py:643
  455.5 16.4 %collective-permute-start.30 = (bf16[6,2,16,128]{3,2,1,0:T(8,128)(2,1)S(1)}, bf16[6,2,16,128]{3,2,1,0:T(8,128)(2,1)S(1)}, u32[]{:S(2)}, u32[]{:S(2)}) collective-permute-start(bf16[6,2,16,128]{3,2,1,0:T(8,128)(2,1)S(1)} %bitcast.83), channel_id=1, source_target_pairs={{0,18},{2,16},{4,22},{6,20},{8,26},{10,24},{12,30},{14,28},{16,2},... | collective-permute-start | bytes 147464 | tf_op jit(solution)/shard_map/ppermute | solution.py:643
  455.8 17.6 %collective-permute-start.31 = (bf16[6,2,16,128]{3,2,1,0:T(8,128)(2,1)S(1)}, bf16[6,2,16,128]{3,2,1,0:T(8,128)(2,1)S(1)}, u32[]{:S(2)}, u32[]{:S(2)}) collective-permute-start(bf16[6,2,16,128]{3,2,1,0:T(8,128)(2,1)S(1)} %bitcast.82), channel_id=1, source_target_pairs={{0,20},{2,22},{4,16},{6,18},{8,28},{10,30},{12,24},{14,26},{16,4},... | collective-permute-start | bytes 147464 | tf_op jit(solution)/shard_map/ppermute | solution.py:643
  471.9 70.9 %collective-permute-start.19 = (bf16[10,2,256,128]{3,2,1,0:T(8,128)(2,1)}, bf16[10,2,256,128]{3,2,1,0:T(8,128)(2,1)S(1)}, u32[]{:S(2)}, u32[]{:S(2)}) collective-permute-start(bf16[10,2,256,128]{3,2,1,0:T(8,128)(2,1)} %get-tuple-element.73), channel_id=1, source_target_pairs={{0,1},{1,0},{2,3},{3,2},{4,5},{5,4},{6,7},{7,6},{8,9},{9,8},{10,11... | collective-permute-start | bytes 3932168 | tf_op jit(solution)/shard_map/ppermute | solution.py:670
  473.4 62.6 %collective-permute-start.10 = (bf16[10,2,256,128]{3,2,1,0:T(8,128)(2,1)}, bf16[10,2,256,128]{3,2,1,0:T(8,128)(2,1)S(1)}, u32[]{:S(2)}, u32[]{:S(2)}) collective-permute-start(bf16[10,2,256,128]{3,2,1,0:T(8,128)(2,1)} %get-tuple-element.63), channel_id=1, source_target_pairs={{0,1},{1,0},{2,3},{3,2},{4,5},{5,4},{6,7},{7,6},{8,9},{9,8},{10,11... | collective-permute-start | bytes 3932168 | tf_op jit(solution)/shard_map/ppermute | solution.py:670
  476.2 22.6 %collective-permute-start = (f32[1,1024,128]{2,1,0:T(8,128)}, f32[1,1024,128]{2,1,0:T(8,128)}, u32[]{:S(2)}, u32[]{:S(2)}) collective-permute-start(f32[1,1024,128]{2,1,0:T(8,128)} %bitcast.3), channel_id=1, source_target_pairs={{0,2},{2,4},{4,6},{6,8},{8,10},{10,12},{12,14},{14,16},{16,18},{18... | collective-permute-start | bytes 1572872 | tf_op jit(solution)/shard_map/ppermute | solution.py:25
  480.7 11.4 %collective-permute-start.36 = (bf16[6,2,16,128]{3,2,1,0:T(8,128)(2,1)}, bf16[6,2,16,128]{3,2,1,0:T(8,128)(2,1)}, u32[]{:S(2)}, u32[]{:S(2)}) collective-permute-start(bf16[6,2,16,128]{3,2,1,0:T(8,128)(2,1)} %bitcast.44), channel_id=1, source_target_pairs={{0,30},{2,28},{4,26},{6,24},{8,22},{10,20},{12,18},{14,16},{16,14}... | collective-permute-start | bytes 147464 | tf_op jit(solution)/shard_map/ppermute | solution.py:643
  490.5 59.1 %collective-permute-start.28 = (bf16[6,2,256,128]{3,2,1,0:T(8,128)(2,1)}, bf16[6,2,256,128]{3,2,1,0:T(8,128)(2,1)S(1)}, u32[]{:S(2)}, u32[]{:S(2)}) collective-permute-start(bf16[6,2,256,128]{3,2,1,0:T(8,128)(2,1)} %get-tuple-element.84), channel_id=1, source_target_pairs={{0,1},{1,0},{2,3},{3,2},{4,5},{5,4},{6,7},{7,6},{8,9},{9,8},{10,11... | collective-permute-start | bytes 2359304 | tf_op jit(solution)/shard_map/ppermute | solution.py:670
  498.2 66.7 %collective-permute-start.37 = (bf16[6,2,256,128]{3,2,1,0:T(8,128)(2,1)}, bf16[6,2,256,128]{3,2,1,0:T(8,128)(2,1)}, u32[]{:S(2)}, u32[]{:S(2)}) collective-permute-start(bf16[6,2,256,128]{3,2,1,0:T(8,128)(2,1)} %get-tuple-element.93), channel_id=1, source_target_pairs={{0,1},{1,0},{2,3},{3,2},{4,5},{5,4},{6,7},{7,6},{8,9},{9,8},{10,11... | collective-permute-start | bytes 2359304 | tf_op jit(solution)/shard_map/ppermute | solution.py:670
  (59 other events, 1415.5 us)

commit v3 on v2

--- a/solution.py
+++ b/solution.py
@@ -151,6 +151,9 @@
     return data_gradient + tv_weight * tv_part
 
 
+PAD = 8
+
+
 def pair_tables(scale, row_order, col_order):
     phase = numpy.outer(row_order, col_order) % NL
     angle = 2.0 * math.pi / NL * phase
@@ -167,6 +170,7 @@
 def rows_kernel(image_ref, maps_ref, cos_ref, sin_ref, out_ref, map_scr, spec_scr):
     half = pl.program_id(1)
     out_rows = cos_ref.shape[0]
+    stride = 2 * out_rows + PAD
     cosine = cos_ref[...]
     sine = sin_ref[...]
     for pair in range(4):
@@ -184,7 +188,7 @@
         spec_real = mxu(cosine, real) + mxu(sine, imag)
         spec_imag = mxu(cosine, imag) - mxu(sine, real)
         for sub in range(2):
-            base = pl.multiple_of((half * 8 + 2 * pair + sub) * 2 * out_rows, 2 * out_rows)
+            base = pl.multiple_of((half * 8 + 2 * pair + sub) * stride, 8)
             lanes = slice(sub * NZ, (sub + 1) * NZ)
             spec_scr[pl.ds(base, out_rows), :] = spec_real[:, lanes]
             spec_scr[pl.ds(base + out_rows, out_rows), :] = spec_imag[:, lanes]
@@ -196,8 +200,8 @@
                 col = step * 8 + sub
                 for part in range(2):
                     start = part * out_rows + col
-                    low = spec_scr[pl.ds(start, 8, 2 * out_rows), :]
-                    high = spec_scr[pl.ds(start + 16 * out_rows, 8, 2 * out_rows), :]
+                    low = spec_scr[pl.ds(start, 8, stride), :]
+                    high = spec_scr[pl.ds(start + 8 * stride, 8, stride), :]
                     out_ref[2 * col + part] = jnp.concatenate([low, high], 0).astype(jnp.bfloat16)
             return carry
 
@@ -220,7 +224,7 @@
         out_shape=jax.ShapeDtypeStruct((2 * out_rows, rows, NZ), jnp.bfloat16),
         scratch_shapes=[
             pltpu.VMEM((8, 2 * NL, NZ), jnp.float32),
-            pltpu.VMEM((16 * 2 * out_rows, NZ), jnp.float32),
+            pltpu.VMEM((16 * (2 * out_rows + PAD), NZ), jnp.float32),
         ],
         cost_estimate=pl.CostEstimate(
             flops=8 * rows * out_rows * NL * NZ, bytes_accessed=30000000, transcendentals=0
@@ -347,14 +351,15 @@
     rows_imag = mxu(sine, back_real) + mxu(cosine, back_imag)
     for col in range(2):
         lanes = slice(col * NZ, (col + 1) * NZ)
-        base = pl.multiple_of((2 * step + col) * 2 * NL, 2 * NL)
+        base = pl.multiple_of((2 * step + col) * (2 * NL + PAD), 8)
         moved[pl.ds(base, NL), :] = rows_real[:, lanes]
         moved[pl.ds(base + NL, NL), :] = rows_imag[:, lanes]
 
     @pl.when(step == steps - 1)
     def _():
         own_rows = spec_ref.shape[2]
-        groups = moved.shape[0] // (16 * NL)
+        stride = 2 * NL + PAD
+        groups = moved.shape[0] // (8 * stride)
         for out, (kind, which, count, base_row, each) in zip(outs, jobs):
             if kind == "cross":
                 base_owner = pen_ref[0] ^ which
@@ -370,7 +375,7 @@
                     start_row = part * NL + source
                     out[2 * row + part] = jnp.concatenate(
                         [
-                            moved[pl.ds(start_row + 16 * NL * group, 8, 2 * NL), :]
+                            moved[pl.ds(start_row + 8 * stride * group, 8, stride), :]
                             for group in range(groups)
                         ],
                         0,
@@ -407,7 +412,7 @@
                 pltpu.VMEM((2 * per_col, TILE, 2 * NZ), jnp.float32),
                 pltpu.VMEM((2, NL, 2 * NZ), jnp.bfloat16),
                 pltpu.VMEM((2, 2 * TILE, NZ), jnp.float32),
-                pltpu.VMEM((cols * 2 * NL, NZ), jnp.float32),
+                pltpu.VMEM((cols * (2 * NL + PAD), NZ), jnp.float32),
                 pltpu.VMEM((DEPTH, TILE, TILE), jnp.bfloat16),
                 pltpu.VMEM((DEPTH, 2 * TILE, NZ), jnp.bfloat16),
                 pltpu.SemaphoreType.DMA((DEPTH,)),
@@ -425,16 +430,16 @@
     )(*plan, spectra, *tables, kernels, samples)
 
 
-def image_kernel(crosses, where_ref, early_ref, near_ref, *rest):
-    cross_refs = rest[: len(crosses)]
-    maps_ref, cos_ref, sin_ref, own_ref, send_ref, map_scr, late = rest[len(crosses) :]
+def image_kernel(where_ref, early_ref, *rest):
+    owners = early_ref.shape[0]
+    late_refs = rest[:owners]
+    maps_ref, cos_ref, sin_ref, own_ref, send_ref, map_scr, late = rest[owners:]
     coil_id = where_ref[0]
     pen_id = where_ref[1]
     cosine = cos_ref[...]
     sine = sin_ref[...]
     cols = early_ref.shape[3]
-    count = early_ref.shape[0] * cols
-    near = near_ref.shape[0]
+    count = owners * cols
     half = NL // 2
     parts = []
     for part in range(2):
@@ -442,13 +447,9 @@
         for row in range(2):
             spot = slice(row * NZ, (row + 1) * NZ)
             lanes.append(early_ref[:, row, part].reshape(count, NZ))
-            base = pl.multiple_of((pen_id & near) * cols, cols)
-            late[part, pl.ds(base, near * cols), spot] = near_ref[:, row, part].reshape(
-                near * cols, NZ
-            )
-            for which, cross_ref in zip(crosses, cross_refs):
+            for which, late_ref in enumerate(late_refs):
                 base = pl.multiple_of((pen_id ^ which) * cols, cols)
-                late[part, pl.ds(base, cols), spot] = cross_ref[row, part]
+                late[part, pl.ds(base, cols), spot] = late_ref[row, part]
         parts.append(jnp.concatenate([jnp.concatenate(lanes, 1), late[part]], 0))
     back_real = mxu(cosine, parts[0]) - mxu(sine, parts[1])
     back_imag = mxu(sine, parts[0]) + mxu(cosine, parts[1])
@@ -472,7 +473,7 @@
                 send_ref[row, 1] = term_imag.astype(jnp.bfloat16)
 
 
-def image_stage(where, early, near, crosses, across, maps, tables, base_row, early_row):
+def image_stage(where, early, across, maps, tables, base_row, early_row):
     each, _, cols = across[0].shape[:3]
     owners = early.shape[0]
     half = NL // 2
@@ -480,16 +481,13 @@
     early_base = early_row // 2
     whole = lambda i, *refs: (0, 0)
     return pl.pallas_call(
-        functools.partial(image_kernel, crosses),
+        image_kernel,
         grid_spec=pltpu.PrefetchScalarGridSpec(
             num_scalar_prefetch=1,
             grid=(each // 2,),
             in_specs=[
                 pl.BlockSpec(
                     (owners, 2, 2, cols, NZ), lambda i, *refs: (0, early_base + i, 0, 0, 0)
-                ),
-                pl.BlockSpec(
-                    (near.shape[0], 2, 2, cols, NZ), lambda i, *refs: (0, base + i, 0, 0, 0)
                 ),
             ]
             + [pl.BlockSpec((2, 2, cols, NZ), lambda i, *refs: (i, 0, 0, 0)) for one in across]
@@ -514,7 +512,7 @@
         cost_estimate=pl.CostEstimate(
             flops=8 * each * NL * NL * NZ, bytes_accessed=each * 1200000, transcendentals=0
         ),
-    )(where, early, near, *across, maps, *tables)
+    )(where, early, *across, maps, *tables)
 
 
 def sum_kernel(total_ref, own_ref, other_ref, out_ref):
@@ -601,11 +599,8 @@
     where = jnp.stack([coil_id, pen_id]).astype(jnp.int32)
     plan = plan + (where[1:],)
     unit = own_rows // 32
-    sizes = [10 * unit, 10 * unit, 6 * unit, 6 * unit]
+    sizes = [10 * unit, 12 * unit, 6 * unit, 4 * unit]
     row_pieces = tuple((sum(sizes[:n]), sizes[n]) for n in range(len(sizes)))
-    near_count = pen_count // 2
-    crosses = tuple(range(near_count, pen_count))
-    near_groups = [list(range(near_count)), list(range(near_count, pen_count))]
     cut = sizes[0] + sizes[1]
     halves = ((0, cut), (cut, own_rows - cut))
 
@@ -622,36 +617,26 @@
     early = []
     for part, (base_row, each) in enumerate(halves):
         early.append(exchange(first[part].reshape(pen_count, each, 2, chunk_cols, NZ)))
-    jobs = [("near", near_count, near_count, 0, own_rows)]
-    for base_row, each in row_pieces:
-        jobs += [("cross", which, 1, base_row, each) for which in crosses]
+    jobs = [
+        ("cross", which, 1, base_row, each)
+        for base_row, each in row_pieces
+        for which in range(pen_count)
+    ]
     result = column_stage(
         arrived[1], tables_cols, kernels, sample_rows, plan, 1, chunks, tuple(jobs)
     )
-    near = lax.all_to_all(
-        result[0].reshape(near_count, own_rows, 2, chunk_cols, NZ),
-        "pen",
-        split_axis=0,
-        concat_axis=0,
-        axis_index_groups=near_groups,
-        tiled=True,
-    )
     across = []
     for piece, (base_row, each) in enumerate(row_pieces):
-        across.append(
-            [
-                lax.ppermute(
-                    result[1 + piece * near_count + place].reshape(each, 2, chunk_cols, NZ),
-                    "pen",
-                    [(i, i ^ which) for i in range(pen_count)],
-                )
-                for place, which in enumerate(crosses)
-            ]
-        )
+        ours = [
+            one.reshape(each, 2, chunk_cols, NZ)
+            for one in result[piece * pen_count : (piece + 1) * pen_count]
+        ]
+        for which in reversed(range(1, pen_count)):
+            pairs = [(i, i ^ which) for i in range(pen_count)]
+            ours[which] = lax.ppermute(ours[which], "pen", pairs)
+        across.append(ours)
     shift = coil_id * (NL // 2)
-    back_cos = jnp.roll(tables_back[0], -shift, 0)
-    later_shift = lax.optimization_barrier((shift, result[-1]))[0]
-    back_sin = jnp.roll(tables_back[1], -later_shift, 0)
+    tables_back = [jnp.roll(table, -shift, 0) for table in tables_back]
     total = variation_stage(image, above, below, where)
     side_maps = maps.reshape(own_rows, 2, NL, NZ)
     for piece, (base_row, each) in enumerate(row_pieces):
@@ -659,11 +644,9 @@
         own, send = image_stage(
             where,
             early[part],
-            near,
-            crosses,
             across[piece],
             side_maps,
-            (back_cos, back_sin),
+            tables_back,
             base_row,
             base_row - halves[part][0],
         )

time: 570 us -> 581 us (1.019)
  Pallas kernels: 225 us -> 204 us
  blocking collectives: 64.6 us -> 84.8 us
  starting transfers between devices: 117 us -> 129 us
    ppermute x32 -> x60, starting transfers between devices: 58.2 us -> 89.4 us  [gradient_parts(): ours[which] = lax.ppermute(ours[which], 'pen', pairs)]
    all_to_all x1, blocking collectives: 64.6 us -> 84.8 us  [exchange(): return lax.all_to_all(array, 'pen', split_axis=0, concat_axis=0, tiled=True)]
    all_to_all x1 -> x0, starting transfers between devices: 18.7 us -> none  [gradient_parts(): lax.all_to_all(result[0].reshape(near_count, own_rows, 2, chunk_cols, NZ)...]
    pallas_call x2, Pallas kernels: 108 us -> 95.2 us  [column_stage(): pl.pallas_call(functools.partial(columns_kernel, chunk * steps, jobs), gr...]
    ppermute x4, waiting for transfers between devices: 10.4 us -> 0.01 us  [gradient_parts(): other = lax.ppermute(send, 'coil', [(0, 1), (1, 0)])]
    all_to_all x3, waiting for transfers between devices: 82 us -> 90.5 us  [exchange(): return lax.all_to_all(array, 'pen', split_axis=0, concat_axis=0, tiled=True)]
    pallas_call x2, Pallas kernels: 35.8 us -> 28.9 us  [row_spectra(): pl.pallas_call(rows_kernel, grid=(rows // 16, 2), in_specs=[pl.BlockSpec(...]
    ppermute x32 -> x60, waiting for transfers between devices: 55.3 us -> 55.4 us  [gradient_parts(): ours[which] = lax.ppermute(ours[which], 'pen', pairs)]
  transfers between devices with their start and end apart: 42 -> 69, of which waited for: 13 -> 18; matrix products, arithmetic and copies ran while one was open for 1% -> 1% of each run, Pallas kernels for 36% -> 32%
where the time goes in v3:
time: 581 us; the launch traced here: 578 us
  Pallas kernels  204 us (35%)
  waiting for transfers between devices  146 us (25%)
  starting transfers between devices  129 us (22%)
  blocking collectives  84.8 us (15%)
  local copies, waits for them, and re-layouts  10.6 us (2%)
    pallas_call x2, Pallas kernels, column_stage(): pl.pallas_call(functools.partial(columns_kernel, chunk * steps, jobs), gr...  95.2 us
    all_to_all x3, waiting for transfers between devices, exchange(): return lax.all_to_all(array, 'pen', split_axis=0, concat_axis=0, tiled=True)  90.5 us
    ppermute x60, starting transfers between devices, gradient_parts(): ours[which] = lax.ppermute(ours[which], 'pen', pairs)  89.4 us
    all_to_all x1, blocking collectives, exchange(): return lax.all_to_all(array, 'pen', split_axis=0, concat_axis=0, tiled=True)  84.8 us
    ppermute x60, waiting for transfers between devices, gradient_parts(): ours[which] = lax.ppermute(ours[which], 'pen', pairs)  55.4 us
    pallas_call x1, Pallas kernels, variation_stage(): pl.pallas_call(variation_kernel, grid_spec=pltpu.PrefetchScalarGridSpec(n...  33.1 us
    all_to_all x3, starting transfers between devices, exchange(): return lax.all_to_all(array, 'pen', split_axis=0, concat_axis=0, tiled=True)  31.4 us
    pallas_call x2, Pallas kernels, row_spectra(): pl.pallas_call(rows_kernel, grid=(rows // 16, 2), in_specs=[pl.BlockSpec(...  28.9 us
  transfers between devices with their start and end apart: 69, of which 18 were waited for; matrix products, arithmetic and copies ran while one was open for 1% of the time, Pallas kernels for 32%

profile of v3, /device:TPU:0, one launch (start us, length us, event | category | flops | bytes accessed | tf_op | source)
XLA Modules:
  0.0 577.7 jit_solution(16056729662943152577)
XLA Ops:
  0.0 14.4 %shard_map.109 = bf16[512,32,128]{2,1,0:T(8,128)(2,1)} custom-call(f32[32,1024,128]{2,1,0:T(8,128)} %bitcast.83, bf16[32,1024,128]{2,1,0:T(8,128)(2,1)} %bitcast.77, bf16[512,512]{1,0:T(8,128)(2,1)} %constant.61.clone.cos_ref, bf16[512,512]{1,0:T(8,128)(2,1)} %constant.62.clone.sin_ref), custom_call_target="tpu_custom_call" | custom-call | flops 4294967296 | bytes 30000000 | tf_op jit(solution)/shard_map/pallas_call | solution.py:214
  14.4 7.4 %all-to-all-start = ((bf16[16,32,32,128]{3,2,1,0:T(8,128)(2,1)}), bf16[16,32,32,128]{3,2,1,0:T(8,128)(2,1)}, u32[]{:S(2)}, u32[]{:S(2)}) async-start(bf16[16,32,32,128]{3,2,1,0:T(8,128)(2,1)} %bitcast.88), calls=%async_computation | async-start | bytes 8388608 | tf_op jit(solution)/shard_map/all_to_all | solution.py:590
  21.9 14.5 %shard_map.111 = bf16[512,32,128]{2,1,0:T(8,128)(2,1)} custom-call(f32[32,1024,128]{2,1,0:T(8,128)} %bitcast.84, bf16[32,1024,128]{2,1,0:T(8,128)(2,1)} %bitcast.78, bf16[512,512]{1,0:T(8,128)(2,1)} %constant.61.clone.cos_ref, bf16[512,512]{1,0:T(8,128)(2,1)} %constant.62.clone.sin_ref), custom_call_target="tpu_custom_call" | custom-call | flops 4294967296 | bytes 30000000 | tf_op jit(solution)/shard_map/pallas_call | solution.py:214
  36.4 63.0 %all-to-all-done.spec_ref = bf16[16,32,32,128]{3,2,1,0:T(8,128)(2,1)} async-done(((bf16[16,32,32,128]{3,2,1,0:T(8,128)(2,1)}), bf16[16,32,32,128]{3,2,1,0:T(8,128)(2,1)}, u32[]{:S(2)}, u32[]{:S(2)}) %all-to-all-start) | async-done | bytes 4194336 | tf_op jit(solution)/shard_map/all_to_all | solution.py:590
  99.4 19.8 %all-to-all-start.2 = ((bf16[16,32,32,128]{3,2,1,0:T(8,128)(2,1)}), bf16[16,32,32,128]{3,2,1,0:T(8,128)(2,1)}, u32[]{:S(2)}, u32[]{:S(2)}) async-start(bf16[16,32,32,128]{3,2,1,0:T(8,128)(2,1)} %bitcast.87), calls=%async_computation.2 | async-start | bytes 8388608 | tf_op jit(solution)/shard_map/all_to_all | solution.py:590
  121.5 47.8 %shard_map.110 = (bf16[704,16,128]{2,1,0:T(8,128)(2,1)}, bf16[320,16,128]{2,1,0:T(8,128)(2,1)}) custom-call(s32[256]{0:T(256)} %get-tuple-element.155.order_ref, s32[256]{0:T(256)} %and_select_fusion.local_ref, s32[17]{0:T(128)} %convert_reduce_fusion.1.bounds_ref, s32[1]{0:T(128)} %bitcast.1.pen_ref, bf16[16,32,32,128]{3,2,1,0:T(8,128)(2,1)} %all-to-all-done.spec_ref, ...), custom_call_target="tpu_custom_call" | custom-call | flops 30000001024 | bytes 20000000 | tf_op jit(solution)/shard_map/pallas_call | solution.py:394
  169.3 27.5 %all-to-all-done.2.spec_ref = bf16[16,32,32,128]{3,2,1,0:T(8,128)(2,1)} async-done(((bf16[16,32,32,128]{3,2,1,0:T(8,128)(2,1)}), bf16[16,32,32,128]{3,2,1,0:T(8,128)(2,1)}, u32[]{:S(2)}, u32[]{:S(2)}) %all-to-all-start.2) | async-done | bytes 4194336 | tf_op jit(solution)/shard_map/all_to_all | solution.py:590
  196.8 84.8 %all_to_all.20.early_ref = bf16[16,22,2,16,128]{4,3,2,1,0:T(8,128)(2,1)} all-to-all(bf16[16,22,2,16,128]{4,3,2,1,0:T(8,128)(2,1)} %bitcast.89), channel_id=1, replica_groups=mesh['pen'=16,'coil'=2] {'pen'}, dimensions={0} | all-to-all | bytes 5767168 | tf_op jit(solution)/shard_map/all_to_all | solution.py:590
  281.6 4.2 all-to-all-start.3
  285.8 47.5 %shard_map.112 = (bf16[20,16,128]{2,1,0:T(8,128)(2,1)}, bf16[20,16,128]{2,1,0:T(8,128)(2,1)}, bf16[20,16,128]{2,1,0:T(8,128)(2,1)}, bf16[20,16,128]{2,1,0:T(8,12...) custom-call(s32[256]{0:T(256)} %get-tuple-element.155.order_ref, ...), custom_call_target="tpu_custom_call" | custom-call | flops 30000001024 | bytes 20000000 | tf_op jit(solution)/shard_map/pallas_call | solution.py:394
  335.7 3.3 collective-permute-start.53
  341.8 3.8 collective-permute-start.57
  350.8 4.7 collective-permute-done.58.rest_9_
  370.3 4.0 collective-permute-done.9.rest_8_
  393.5 7.9 %collective-permute-done.26.rest_9_ = bf16[12,2,16,128]{3,2,1,0:T(8,128)(2,1)} collective-permute-done((bf16[12,2,16,128]{3,2,1,0:T(8,128)(2,1)}, bf16[12,2,16,128]{3,2,1,0:T(8,128)(2,1)}, u32[]{:S(2)}, u32[]{:S(2)}) %collective-permute-start.26) | collective-permute-done | bytes 98336 | tf_op jit(solution)/shard_map/ppermute | solution.py:636
  414.6 9.3 %shard_map.115 = (f32[12,2,256,128]{3,2,1,0:T(8,128)}, bf16[12,2,256,128]{3,2,1,0:T(8,128)(2,1)}) custom-call(s32[2]{0:T(128)} %pad_add_fusion.where_ref, bf16[16,22,2,16,128]{4,3,2,1,0:T(8,128)(2,1)} %all_to_all.20.early_ref, bf16[12,2,16,128]{3,2,1,0:T(8,128)(2,1)} %bitcast.91, bf16[12,2,16,128]{3,2,1,0:T(8,128)(2,1)} %copy-done.7, ...), custom_call_target="tpu_custom_call" | custom-call | flops 3221225472 | bytes 14400000 | tf_op jit(solution)/shard_map/pallas_call | solution.py:483
  424.0 5.4 collective-permute-done.12.rest_11_
  430.9 9.1 %collective-permute-start.38 = (bf16[6,2,16,128]{3,2,1,0:T(8,128)(2,1)}, bf16[6,2,16,128]{3,2,1,0:T(8,128)(2,1)S(1)}, u32[]{:S(2)}, u32[]{:S(2)}) collective-permute-start(bf16[6,2,16,128]{3,2,1,0:T(8,128)(2,1)} %bitcast.49), channel_id=1, source_target_pairs={{0,10},{2,8},{4,14},{6,12},{8,2},{10,0},{12,6},{14,4},{16,26},{18,... | collective-permute-start | bytes 147464 | tf_op jit(solution)/shard_map/ppermute | solution.py:636
  443.2 8.3 %shard_map.113 = (f32[10,2,256,128]{3,2,1,0:T(8,128)}, bf16[10,2,256,128]{3,2,1,0:T(8,128)(2,1)}) custom-call(s32[2]{0:T(128)} %pad_add_fusion.where_ref, bf16[16,22,2,16,128]{4,3,2,1,0:T(8,128)(2,1)} %all_to_all.20.early_ref, bf16[10,2,16,128]{3,2,1,0:T(8,128)(2,1)} %bitcast.92, bf16[10,2,16,128]{3,2,1,0:T(8,128)(2,1)} %copy-done.13, ...), custom_call_target="tpu_custom_call" | custom-call | flops 2684354560 | bytes 12000000 | tf_op jit(solution)/shard_map/pallas_call | solution.py:483
  471.3 3.6 collective-permute-start.48
  475.7 4.2 collective-permute-start.59
  480.5 2.8 collective-permute-start.60
  484.4 6.1 %shard_map.117 = (f32[6,2,256,128]{3,2,1,0:T(8,128)}, bf16[6,2,256,128]{3,2,1,0:T(8,128)(2,1)}) custom-call(s32[2]{0:T(128)} %pad_add_fusion.where_ref, bf16[16,10,2,16,128]{4,3,2,1,0:T(8,128)(2,1)} %copy-done, bf16[6,2,16,128]{3,2,1,0:T(8,128)(2,1)} %bitcast.93, bf16[6,2,16,128]{3,2,1,0:T(8,128)(2,1)} %copy-done.26, bf16[6,2,16,128]{3,2,1,0:T(8,128)(2,1)} %copy-done.27, ...), custom_call_target="tpu_custom_call" | custom-call | flops 1610612736 | bytes 7200000 | tf_op jit(solution)/shard_map/pallas_call | solution.py:483
  492.3 5.8 %collective-permute-done.61.rest_12_ = bf16[4,2,16,128]{3,2,1,0:T(8,128)(2,1)S(1)} collective-permute-done((bf16[4,2,16,128]{3,2,1,0:T(8,128)(2,1)}, bf16[4,2,16,128]{3,2,1,0:T(8,128)(2,1)S(1)}, u32[]{:S(2)}, u32[]{:S(2)}) %collective-permute-start.61) | collective-permute-done | bytes 32800 | tf_op jit(solution)/shard_map/ppermute | solution.py:636
  498.1 5.3 collective-permute-done.62.rest_13_
  506.1 4.2 collective-permute-done.63.rest_14_
  510.3 6.2 %collective-permute-done.64.rest_15_ = bf16[4,2,16,128]{3,2,1,0:T(8,128)(2,1)S(1)} collective-permute-done((bf16[4,2,16,128]{3,2,1,0:T(8,128)(2,1)}, bf16[4,2,16,128]{3,2,1,0:T(8,128)(2,1)S(1)}, u32[]{:S(2)}, u32[]{:S(2)}) %collective-permute-start.64) | collective-permute-done | bytes 32800 | tf_op jit(solution)/shard_map/ppermute | solution.py:636
  517.8 4.7 shard_map.119
  524.1 33.1 %variation.1.total_ref = f32[32,512,128]{2,1,0:T(8,128)} custom-call(s32[2]{0:T(128)} %pad_add_fusion.where_ref, f32[32,1024,128]{2,1,0:T(8,128)} %bitcast.85, f32[32,1024,128]{2,1,0:T(8,128)} %bitcast.86, f32[1,1024,128]{2,1,0:T(8,128)} %copy-done.3, f32[1,1024,128]{2,1,0:T(8,128)} %copy-done.4), custom_call_target="tpu_custom_call" | custom-call | flops 83886080 | bytes 60000000 | tf_op jit(solution)/shard_map/variation/pallas_call | solution.py:753
  557.3 5.7 shard_map.114.total_ref
  564.2 6.1 %shard_map.116.total_ref = f32[32,512,128]{2,1,0:T(8,128)} custom-call(f32[32,512,128]{2,1,0:T(8,128)} %shard_map.114.total_ref, f32[12,2,256,128]{3,2,1,0:T(8,128)} %get-tuple-element.115.own_ref, bf16[12,2,256,128]{3,2,1,0:T(8,128)(2,1)} %copy-done.1), custom_call_target="tpu_custom_call", output_to_operand_aliasing={{}: (0, {})} | custom-call | flops 1572864 | bytes 12000000 | tf_op jit(solution)/shard_map/pallas_call | solution.py:532
  571.2 3.9 shard_map.118.total_ref
  (239 shorter events, 98.4 us)
Async XLA Ops:
  14.4 85.0 %all-to-all-start = ((bf16[16,32,32,128]{3,2,1,0:T(8,128)(2,1)}), bf16[16,32,32,128]{3,2,1,0:T(8,128)(2,1)}, u32[]{:S(2)}, u32[]{:S(2)}) async-start(bf16[16,32,32,128]{3,2,1,0:T(8,128)(2,1)} %bitcast.88), calls=%async_computation | async-start | bytes 8388608 | tf_op jit(solution)/shard_map/all_to_all | solution.py:590
  99.4 97.4 %all-to-all-start.2 = ((bf16[16,32,32,128]{3,2,1,0:T(8,128)(2,1)}), bf16[16,32,32,128]{3,2,1,0:T(8,128)(2,1)}, u32[]{:S(2)}, u32[]{:S(2)}) async-start(bf16[16,32,32,128]{3,2,1,0:T(8,128)(2,1)} %bitcast.87), calls=%async_computation.2 | async-start | bytes 8388608 | tf_op jit(solution)/shard_map/all_to_all | solution.py:590
  281.6 201.8 %all-to-all-start.3 = ((bf16[16,10,2,16,128]{4,3,2,1,0:T(8,128)(2,1)}), bf16[16,10,2,16,128]{4,3,2,1,0:T(8,128)(2,1)S(1)}, u32[]{:S(2)}, u32[]{:S(2)}) async-start(bf16[16,10,2,16,128]{4,3,2,1,0:T(8,128)(2,1)} %bitcast.43), calls=%async_computation.3 | async-start | bytes 2621440 | tf_op jit(solution)/shard_map/all_to_all | solution.py:590
  346.6 10.1 %collective-permute-start.35 = (bf16[6,2,16,128]{3,2,1,0:T(8,128)(2,1)}, bf16[6,2,16,128]{3,2,1,0:T(8,128)(2,1)S(1)}, u32[]{:S(2)}, u32[]{:S(2)}) collective-permute-start(bf16[6,2,16,128]{3,2,1,0:T(8,128)(2,1)} %bitcast.137), channel_id=1, source_target_pairs={{0,4},{2,6},{4,0},{6,2},{8,12},{10,14},{12,8},{14,10},{16,20},{18,... | collective-permute-start | bytes 147464 | tf_op jit(solution)/shard_map/ppermute | solution.py:636
  362.6 11.7 %collective-permute-start.9 = (bf16[10,2,16,128]{3,2,1,0:T(8,128)(2,1)}, bf16[10,2,16,128]{3,2,1,0:T(8,128)(2,1)S(1)}, u32[]{:S(2)}, u32[]{:S(2)}) collective-permute-start(bf16[10,2,16,128]{3,2,1,0:T(8,128)(2,1)} %bitcast.119), channel_id=1, source_target_pairs={{0,16},{2,18},{4,20},{6,22},{8,24},{10,26},{12,28},{14,30},{16,0},... | collective-permute-start | bytes 245768 | tf_op jit(solution)/shard_map/ppermute | solution.py:636
  363.5 11.5 %collective-permute-start.10 = (bf16[10,2,16,128]{3,2,1,0:T(8,128)(2,1)}, bf16[10,2,16,128]{3,2,1,0:T(8,128)(2,1)}, u32[]{:S(2)}, u32[]{:S(2)}) collective-permute-start(bf16[10,2,16,128]{3,2,1,0:T(8,128)(2,1)} %bitcast.118), channel_id=1, source_target_pairs={{0,18},{2,16},{4,22},{6,20},{8,26},{10,24},{12,30},{14,28},{16,2},... | collective-permute-start | bytes 245768 | tf_op jit(solution)/shard_map/ppermute | solution.py:636
  365.2 12.5 %collective-permute-start.11 = (bf16[10,2,16,128]{3,2,1,0:T(8,128)(2,1)}, bf16[10,2,16,128]{3,2,1,0:T(8,128)(2,1)}, u32[]{:S(2)}, u32[]{:S(2)}) collective-permute-start(bf16[10,2,16,128]{3,2,1,0:T(8,128)(2,1)} %bitcast.117), channel_id=1, source_target_pairs={{0,20},{2,22},{4,16},{6,18},{8,28},{10,30},{12,24},{14,26},{16,4},... | collective-permute-start | bytes 245768 | tf_op jit(solution)/shard_map/ppermute | solution.py:636
  367.1 10.7 %collective-permute-start.18 = (bf16[12,2,16,128]{3,2,1,0:T(8,128)(2,1)}, bf16[12,2,16,128]{3,2,1,0:T(8,128)(2,1)S(1)}, u32[]{:S(2)}, u32[]{:S(2)}) collective-permute-start(bf16[12,2,16,128]{3,2,1,0:T(8,128)(2,1)} %bitcast.111), channel_id=1, source_target_pairs={{0,2},{2,0},{4,6},{6,4},{8,10},{10,8},{12,14},{14,12},{16,18},{18,... | collective-permute-start | bytes 294920 | tf_op jit(solution)/shard_map/ppermute | solution.py:636
  369.0 10.4 %collective-permute-start.19 = (bf16[12,2,16,128]{3,2,1,0:T(8,128)(2,1)}, bf16[12,2,16,128]{3,2,1,0:T(8,128)(2,1)}, u32[]{:S(2)}, u32[]{:S(2)}) collective-permute-start(bf16[12,2,16,128]{3,2,1,0:T(8,128)(2,1)} %bitcast.110), channel_id=1, source_target_pairs={{0,4},{2,6},{4,0},{6,2},{8,12},{10,14},{12,8},{14,10},{16,20},{18,... | collective-permute-start | bytes 294920 | tf_op jit(solution)/shard_map/ppermute | solution.py:636
  379.4 10.9 %collective-permute-start.24 = (bf16[12,2,16,128]{3,2,1,0:T(8,128)(2,1)}, bf16[12,2,16,128]{3,2,1,0:T(8,128)(2,1)}, u32[]{:S(2)}, u32[]{:S(2)}) collective-permute-start(bf16[12,2,16,128]{3,2,1,0:T(8,128)(2,1)} %bitcast.105), channel_id=1, source_target_pairs={{0,14},{2,12},{4,10},{6,8},{8,6},{10,4},{12,2},{14,0},{16,30},{18,... | collective-permute-start | bytes 294920 | tf_op jit(solution)/shard_map/ppermute | solution.py:636
  380.1 12.4 %collective-permute-start.25 = (bf16[12,2,16,128]{3,2,1,0:T(8,128)(2,1)}, bf16[12,2,16,128]{3,2,1,0:T(8,128)(2,1)}, u32[]{:S(2)}, u32[]{:S(2)}) collective-permute-start(bf16[12,2,16,128]{3,2,1,0:T(8,128)(2,1)} %bitcast.104), channel_id=1, source_target_pairs={{0,16},{2,18},{4,20},{6,22},{8,24},{10,26},{12,28},{14,30},{16,0},... | collective-permute-start | bytes 294920 | tf_op jit(solution)/shard_map/ppermute | solution.py:636
  382.1 19.3 %collective-permute-start.26 = (bf16[12,2,16,128]{3,2,1,0:T(8,128)(2,1)}, bf16[12,2,16,128]{3,2,1,0:T(8,128)(2,1)}, u32[]{:S(2)}, u32[]{:S(2)}) collective-permute-start(bf16[12,2,16,128]{3,2,1,0:T(8,128)(2,1)} %bitcast.103), channel_id=1, source_target_pairs={{0,18},{2,16},{4,22},{6,20},{8,26},{10,24},{12,30},{14,28},{16,2},... | collective-permute-start | bytes 294920 | tf_op jit(solution)/shard_map/ppermute | solution.py:636
  383.2 21.0 %collective-permute-start.27 = (bf16[12,2,16,128]{3,2,1,0:T(8,128)(2,1)}, bf16[12,2,16,128]{3,2,1,0:T(8,128)(2,1)}, u32[]{:S(2)}, u32[]{:S(2)}) collective-permute-start(bf16[12,2,16,128]{3,2,1,0:T(8,128)(2,1)} %bitcast.102), channel_id=1, source_target_pairs={{0,20},{2,22},{4,16},{6,18},{8,28},{10,30},{12,24},{14,26},{16,4},... | collective-permute-start | bytes 294920 | tf_op jit(solution)/shard_map/ppermute | solution.py:636
  387.7 18.8 %collective-permute-start.28 = (bf16[12,2,16,128]{3,2,1,0:T(8,128)(2,1)}, bf16[12,2,16,128]{3,2,1,0:T(8,128)(2,1)S(1)}, u32[]{:S(2)}, u32[]{:S(2)}) collective-permute-start(bf16[12,2,16,128]{3,2,1,0:T(8,128)(2,1)} %bitcast.101), channel_id=1, source_target_pairs={{0,22},{2,20},{4,18},{6,16},{8,30},{10,28},{12,26},{14,24},{16,6},... | collective-permute-start | bytes 294920 | tf_op jit(solution)/shard_map/ppermute | solution.py:636
  390.3 16.2 %collective-permute-start.29 = (bf16[12,2,16,128]{3,2,1,0:T(8,128)(2,1)}, bf16[12,2,16,128]{3,2,1,0:T(8,128)(2,1)S(1)}, u32[]{:S(2)}, u32[]{:S(2)}) collective-permute-start(bf16[12,2,16,128]{3,2,1,0:T(8,128)(2,1)} %bitcast.100), channel_id=1, source_target_pairs={{0,24},{2,26},{4,28},{6,30},{8,16},{10,18},{12,20},{14,22},{16,8},... | collective-permute-start | bytes 294920 | tf_op jit(solution)/shard_map/ppermute | solution.py:636
  392.5 16.2 %collective-permute-start.30 = (bf16[12,2,16,128]{3,2,1,0:T(8,128)(2,1)}, bf16[12,2,16,128]{3,2,1,0:T(8,128)(2,1)S(1)}, u32[]{:S(2)}, u32[]{:S(2)}) collective-permute-start(bf16[12,2,16,128]{3,2,1,0:T(8,128)(2,1)} %bitcast.99), channel_id=1, source_target_pairs={{0,26},{2,24},{4,30},{6,28},{8,18},{10,16},{12,22},{14,20},{16,10}... | collective-permute-start | bytes 294920 | tf_op jit(solution)/shard_map/ppermute | solution.py:636
  406.5 22.9 %collective-permute-start.12 = (bf16[10,2,16,128]{3,2,1,0:T(8,128)(2,1)}, bf16[10,2,16,128]{3,2,1,0:T(8,128)(2,1)S(1)}, u32[]{:S(2)}, u32[]{:S(2)}) collective-permute-start(bf16[10,2,16,128]{3,2,1,0:T(8,128)(2,1)} %bitcast.116), channel_id=1, source_target_pairs={{0,22},{2,20},{4,18},{6,16},{8,30},{10,28},{12,26},{14,24},{16,6},... | collective-permute-start | bytes 245768 | tf_op jit(solution)/shard_map/ppermute | solution.py:636
  406.5 24.4 %collective-permute-start.13 = (bf16[10,2,16,128]{3,2,1,0:T(8,128)(2,1)}, bf16[10,2,16,128]{3,2,1,0:T(8,128)(2,1)S(1)}, u32[]{:S(2)}, u32[]{:S(2)}) collective-permute-start(bf16[10,2,16,128]{3,2,1,0:T(8,128)(2,1)} %bitcast.115), channel_id=1, source_target_pairs={{0,24},{2,26},{4,28},{6,30},{8,16},{10,18},{12,20},{14,22},{16,8},... | collective-permute-start | bytes 245768 | tf_op jit(solution)/shard_map/ppermute | solution.py:636
  408.7 31.3 %collective-permute-start.14 = (bf16[10,2,16,128]{3,2,1,0:T(8,128)(2,1)}, bf16[10,2,16,128]{3,2,1,0:T(8,128)(2,1)S(1)}, u32[]{:S(2)}, u32[]{:S(2)}) collective-permute-start(bf16[10,2,16,128]{3,2,1,0:T(8,128)(2,1)} %bitcast.114), channel_id=1, source_target_pairs={{0,26},{2,24},{4,30},{6,28},{8,18},{10,16},{12,22},{14,20},{16,10}... | collective-permute-start | bytes 245768 | tf_op jit(solution)/shard_map/ppermute | solution.py:636
  410.1 30.9 %collective-permute-start.15 = (bf16[10,2,16,128]{3,2,1,0:T(8,128)(2,1)}, bf16[10,2,16,128]{3,2,1,0:T(8,128)(2,1)S(1)}, u32[]{:S(2)}, u32[]{:S(2)}) collective-permute-start(bf16[10,2,16,128]{3,2,1,0:T(8,128)(2,1)} %bitcast.113), channel_id=1, source_target_pairs={{0,28},{2,30},{4,24},{6,26},{8,20},{10,22},{12,16},{14,18},{16,12}... | collective-permute-start | bytes 245768 | tf_op jit(solution)/shard_map/ppermute | solution.py:636
  412.9 29.3 %collective-permute-start.16 = (bf16[10,2,16,128]{3,2,1,0:T(8,128)(2,1)}, bf16[10,2,16,128]{3,2,1,0:T(8,128)(2,1)S(1)}, u32[]{:S(2)}, u32[]{:S(2)}) collective-permute-start(bf16[10,2,16,128]{3,2,1,0:T(8,128)(2,1)} %bitcast.112), channel_id=1, source_target_pairs={{0,30},{2,28},{4,26},{6,24},{8,22},{10,20},{12,18},{14,16},{16,14}... | collective-permute-start | bytes 245768 | tf_op jit(solution)/shard_map/ppermute | solution.py:636
  429.4 133.6 %collective-permute-start.33 = (bf16[12,2,256,128]{3,2,1,0:T(8,128)(2,1)}, bf16[12,2,256,128]{3,2,1,0:T(8,128)(2,1)S(1)}, u32[]{:S(2)}, u32[]{:S(2)}) collective-permute-start(bf16[12,2,256,128]{3,2,1,0:T(8,128)(2,1)} %get-tuple-element.116), channel_id=1, source_target_pairs={{0,1},{1,0},{2,3},{3,2},{4,5},{5,4},{6,7},{7,6},{8,9},{9,8},{10,11... | collective-permute-start | bytes 4718600 | tf_op jit(solution)/shard_map/ppermute | solution.py:653
  430.9 20.6 %collective-permute-start.38 = (bf16[6,2,16,128]{3,2,1,0:T(8,128)(2,1)}, bf16[6,2,16,128]{3,2,1,0:T(8,128)(2,1)S(1)}, u32[]{:S(2)}, u32[]{:S(2)}) collective-permute-start(bf16[6,2,16,128]{3,2,1,0:T(8,128)(2,1)} %bitcast.49), channel_id=1, source_target_pairs={{0,10},{2,8},{4,14},{6,12},{8,2},{10,0},{12,6},{14,4},{16,26},{18,... | collective-permute-start | bytes 147464 | tf_op jit(solution)/shard_map/ppermute | solution.py:636
  440.0 13.8 %collective-permute-start.39 = (bf16[6,2,16,128]{3,2,1,0:T(8,128)(2,1)}, bf16[6,2,16,128]{3,2,1,0:T(8,128)(2,1)S(1)}, u32[]{:S(2)}, u32[]{:S(2)}) collective-permute-start(bf16[6,2,16,128]{3,2,1,0:T(8,128)(2,1)} %bitcast.50), channel_id=1, source_target_pairs={{0,12},{2,14},{4,8},{6,10},{8,4},{10,6},{12,0},{14,2},{16,28},{18,... | collective-permute-start | bytes 147464 | tf_op jit(solution)/shard_map/ppermute | solution.py:636
  441.0 14.3 %collective-permute-start.40 = (bf16[6,2,16,128]{3,2,1,0:T(8,128)(2,1)}, bf16[6,2,16,128]{3,2,1,0:T(8,128)(2,1)S(1)}, u32[]{:S(2)}, u32[]{:S(2)}) collective-permute-start(bf16[6,2,16,128]{3,2,1,0:T(8,128)(2,1)} %bitcast.51), channel_id=1, source_target_pairs={{0,14},{2,12},{4,10},{6,8},{8,6},{10,4},{12,2},{14,0},{16,30},{18,... | collective-permute-start | bytes 147464 | tf_op jit(solution)/shard_map/ppermute | solution.py:636
  442.2 14.7 %collective-permute-start.41 = (bf16[6,2,16,128]{3,2,1,0:T(8,128)(2,1)}, bf16[6,2,16,128]{3,2,1,0:T(8,128)(2,1)S(1)}, u32[]{:S(2)}, u32[]{:S(2)}) collective-permute-start(bf16[6,2,16,128]{3,2,1,0:T(8,128)(2,1)} %bitcast.134), channel_id=1, source_target_pairs={{0,16},{2,18},{4,20},{6,22},{8,24},{10,26},{12,28},{14,30},{16,0},... | collective-permute-start | bytes 147464 | tf_op jit(solution)/shard_map/ppermute | solution.py:636
  456.8 100.5 %collective-permute-start.17 = (bf16[10,2,256,128]{3,2,1,0:T(8,128)(2,1)}, bf16[10,2,256,128]{3,2,1,0:T(8,128)(2,1)}, u32[]{:S(2)}, u32[]{:S(2)}) collective-permute-start(bf16[10,2,256,128]{3,2,1,0:T(8,128)(2,1)} %get-tuple-element.98), channel_id=1, source_target_pairs={{0,1},{1,0},{2,3},{3,2},{4,5},{5,4},{6,7},{7,6},{8,9},{9,8},{10,11... | collective-permute-start | bytes 3932168 | tf_op jit(solution)/shard_map/ppermute | solution.py:653
  459.6 62.9 %collective-permute-start = (f32[1,1024,128]{2,1,0:T(8,128)}, f32[1,1024,128]{2,1,0:T(8,128)S(1)}, u32[]{:S(2)}, u32[]{:S(2)}) collective-permute-start(f32[1,1024,128]{2,1,0:T(8,128)} %bitcast.3), channel_id=1, source_target_pairs={{0,2},{2,4},{4,6},{6,8},{8,10},{10,12},{12,14},{14,16},{16,18},{18... | collective-permute-start | bytes 1572872 | tf_op jit(solution)/shard_map/ppermute | solution.py:25
  475.7 14.8 %collective-permute-start.59 = (bf16[4,2,16,128]{3,2,1,0:T(8,128)(2,1)}, bf16[4,2,16,128]{3,2,1,0:T(8,128)(2,1)}, u32[]{:S(2)}, u32[]{:S(2)}) collective-permute-start(bf16[4,2,16,128]{3,2,1,0:T(8,128)(2,1)} %bitcast.144), channel_id=1, source_target_pairs={{0,20},{2,22},{4,16},{6,18},{8,28},{10,30},{12,24},{14,26},{16,4},... | collective-permute-start | bytes 98312 | tf_op jit(solution)/shard_map/ppermute | solution.py:636
  480.5 11.6 %collective-permute-start.60 = (bf16[4,2,16,128]{3,2,1,0:T(8,128)(2,1)}, bf16[4,2,16,128]{3,2,1,0:T(8,128)(2,1)}, u32[]{:S(2)}, u32[]{:S(2)}) collective-permute-start(bf16[4,2,16,128]{3,2,1,0:T(8,128)(2,1)} %bitcast.143), channel_id=1, source_target_pairs={{0,22},{2,20},{4,18},{6,16},{8,30},{10,28},{12,26},{14,24},{16,6},... | collective-permute-start | bytes 98312 | tf_op jit(solution)/shard_map/ppermute | solution.py:636
  490.6 79.8 %collective-permute-start.49 = (bf16[6,2,256,128]{3,2,1,0:T(8,128)(2,1)}, bf16[6,2,256,128]{3,2,1,0:T(8,128)(2,1)S(1)}, u32[]{:S(2)}, u32[]{:S(2)}) collective-permute-start(bf16[6,2,256,128]{3,2,1,0:T(8,128)(2,1)} %get-tuple-element.135), channel_id=1, source_target_pairs={{0,1},{1,0},{2,3},{3,2},{4,5},{5,4},{6,7},{7,6},{8,9},{9,8},{10,11... | collective-permute-start | bytes 2359304 | tf_op jit(solution)/shard_map/ppermute | solution.py:653
  522.6 52.6 %collective-permute-start.65 = (bf16[4,2,256,128]{3,2,1,0:T(8,128)(2,1)}, bf16[4,2,256,128]{3,2,1,0:T(8,128)(2,1)}, u32[]{:S(2)}, u32[]{:S(2)}) collective-permute-start(bf16[4,2,256,128]{3,2,1,0:T(8,128)(2,1)} %get-tuple-element.153), channel_id=1, source_target_pairs={{0,1},{1,0},{2,3},{3,2},{4,5},{5,4},{6,7},{7,6},{8,9},{9,8},{10,11... | collective-permute-start | bytes 1572872 | tf_op jit(solution)/shard_map/ppermute | solution.py:653
  (92 other events, 1001.9 us)
